TPU v7x, 32 devices: a whole 2x2x4 slice. The times are simulated.
32 devices in a mesh: mem: 8 (over z, x), grp: 4 (over y, core).
Axes of the slice: x: 2, y: 2, z: 4, core: 2. Of those that a mesh axis runs over, the one named last changes fastest.
Arguments:
- prior_members: bfloat16 [256, 32, 256], P('mem', 'grp'), may hold values from -6 to 6
- mapped_prior: bfloat16 [256, 32, 1024], P('mem', 'grp'), may hold values from -6 to 6
- departure: float32 [32, 1024], P(('grp', 'mem')), may hold values from -18 to 18
- precision_factor: float32 [32, 1024], P(('grp', 'mem')), may hold values from 0.02 to 0.5
- measured_lines: int32 [32], P(('grp', 'mem')), may hold values from 256 to 1024, as said below
Outputs:
- analysis: bfloat16 [256, 32, 256], P('mem', 'grp')
Inputs may be any that keep to these rules, and one draw needn't show every extreme that they name: Only the first measured_lines rows of a patch's observation block are used; some patch has exactly 1024 rows and some exactly 256.
All inputs are finite; a program needn't handle non-finite values.
Results may differ from a plain program's by a relative error of at most 0.008.
Values may be sent and summed in bfloat16 or wider, within the bound.
No kernel may reach another device: no remote copies, remote signals or barrier semaphores. Data moves between devices by JAX's collectives and lax.ppermute only.
A program may use at most 64 MiB of HBM per device.

v0:
```python
import math

import jax
import jax.numpy as jnp
from jax import lax
from jax.sharding import PartitionSpec as P

OBS_BLK = 128
ITERS = 5


highest = lax.Precision.HIGHEST


def block_terms(totals, obs_piece, weight_blk, innov_blk, first_row, lines_in_play):
    gram_total, pull_vec = totals
    values = obs_piece.astype(jnp.float32)
    deviat = values - jnp.mean(values, axis=0, keepdims=True)
    row_ids = first_row + jnp.arange(obs_piece.shape[1], dtype=jnp.int32)
    weights = jnp.where(row_ids < lines_in_play, weight_blk, jnp.float32(0.0))
    weighted = deviat * weights[None, :]
    gram_total = gram_total + jnp.dot(weighted, deviat.T, precision=highest)
    pull_vec = pull_vec + jnp.dot(weighted, innov_blk, precision=highest)
    return (gram_total, pull_vec)


def empty_terms(members):
    return (jnp.zeros((members, members), jnp.float32), jnp.zeros((members,), jnp.float32))


def own_terms(measurement_data, departure, precision_factor, measured_lines):
    members = measurement_data.shape[0]

    def patch_terms(domain_number):
        lines_in_play = measured_lines[domain_number]
        column = lax.dynamic_index_in_dim(measurement_data, domain_number, 1, keepdims=False)
        departure_line = lax.dynamic_index_in_dim(departure, domain_number, 0, keepdims=False)
        line_precision_list = lax.dynamic_index_in_dim(
            precision_factor, domain_number, 0, keepdims=False
        )
        blocks_due = (lines_in_play + OBS_BLK - 1) // OBS_BLK

        def block_step(block_no, totals):
            first_row = block_no * OBS_BLK
            obs_piece = lax.dynamic_slice_in_dim(column, first_row, OBS_BLK, 1)
            weight_blk = lax.dynamic_slice_in_dim(line_precision_list, first_row, OBS_BLK, 0)
            innov_blk = lax.dynamic_slice_in_dim(departure_line, first_row, OBS_BLK, 0)
            return block_terms(totals, obs_piece, weight_blk, innov_blk, first_row, lines_in_play)

        return lax.fori_loop(0, blocks_due, block_step, empty_terms(members))

    return lax.map(patch_terms, jnp.arange(measurement_data.shape[1], dtype=jnp.int32))


def finish(gram_total, pull_vec, patch_state):
    members = gram_total.shape[1]
    identity = jnp.eye(members, dtype=jnp.float32)
    system = gram_total + jnp.float32(members - 1) * identity[None]
    fro_scale = jnp.sqrt(jnp.sum(system * system, axis=(1, 2)))
    iterate = system / fro_scale[:, None, None]
    inv_root = jnp.broadcast_to(identity, system.shape)
    for sweep in range(ITERS):
        factor = 0.5 * (
            3.0 * identity[None] - jnp.einsum("pij,pjk->pik", inv_root, iterate, precision=highest)
        )
        iterate = jnp.einsum("pij,pjk->pik", iterate, factor, precision=highest)
        inv_root = jnp.einsum("pij,pjk->pik", factor, inv_root, precision=highest)
    inner = jnp.einsum("pij,pj->pi", inv_root, pull_vec, precision=highest)
    mean_shift = jnp.einsum("pij,pj->pi", inv_root, inner, precision=highest) / fro_scale[:, None]
    transform = (math.sqrt(members - 1) / jnp.sqrt(fro_scale))[
        :, None, None
    ] * inv_root + mean_shift[:, :, None]
    grid_quantities = patch_state.astype(jnp.float32)
    center = jnp.mean(grid_quantities, axis=0, keepdims=True)
    spread = grid_quantities - center
    result = center + jnp.einsum("kpv,pkl->lpv", spread, transform, precision=highest)
    return result.astype(jnp.bfloat16)


def local(prior_members, mapped_prior, departure, precision_factor, measured_lines):
    patch_state, measurement_data = (
        lax.all_to_all(prior_members, "mem", split_axis=1, concat_axis=0, tiled=True),
        lax.all_to_all(mapped_prior, "mem", split_axis=1, concat_axis=0, tiled=True),
    )
    gram_total, pull_vec = own_terms(measurement_data, departure, precision_factor, measured_lines)
    analysed = finish(gram_total, pull_vec, patch_state)
    return lax.all_to_all(analysed, "mem", split_axis=0, concat_axis=1, tiled=True)


def solution(mesh):
    in_specs = (
        P("mem", "grp", None),
        P("mem", "grp", None),
        P(("grp", "mem"), None),
        P(("grp", "mem"), None),
        P(("grp", "mem")),
    )
    out_specs = P("mem", "grp", None)
    return jax.shard_map(local, mesh=mesh, in_specs=in_specs, out_specs=out_specs, check_vma=False)
```

profile of v0, /device:TPU:0, one launch (start us, length us, event | category | flops | bytes accessed | tf_op | source)
XLA Modules:
  0.0 75.7 jit_solution(8132653353621279934)
XLA Ops:
  0.0 1.6 %copy.13 = bf16[32,8,256]{2,0,1:T(8,128)(2,1)} copy(bf16[32,8,256]{2,1,0:T(8,128)(2,1)} %param.7) | data formatting | bytes 262144 | tf_op args[0]
  1.6 7.3 %all-to-all-start = ((bf16[32,8,256]{2,0,1:T(8,128)(2,1)}), bf16[32,8,256]{2,0,1:T(8,128)(2,1)S(1)}, u32[]{:S(2)}, u32[]{:S(2)}) async-start(bf16[32,8,256]{2,0,1:T(8,128)(2,1)} %copy.13), calls=%async_computation | async-start | bytes 262144 | tf_op jit(solution)/shard_map/all_to_all | solution.py:82
  8.9 2.1 %copy.14 = bf16[32,8,1024]{2,0,1:T(8,128)(2,1)} copy(bf16[32,8,1024]{2,1,0:T(8,128)(2,1)} %param.8) | data formatting | bytes 1048576 | tf_op args[1]
  11.0 5.2 %all-to-all-done = bf16[32,8,256]{2,0,1:T(8,128)(2,1)S(1)} async-done(((bf16[32,8,256]{2,0,1:T(8,128)(2,1)}), bf16[32,8,256]{2,0,1:T(8,128)(2,1)S(1)}, u32[]{:S(2)}, u32[]{:S(2)}) %all-to-all-start) | async-done | bytes 131104 | tf_op jit(solution)/shard_map/all_to_all | solution.py:82
  16.2 3.5 %all-to-all-start.1 = ((bf16[32,8,1024]{2,0,1:T(8,128)(2,1)}), bf16[32,8,1024]{2,0,1:T(8,128)(2,1)S(1)}, u32[]{:S(2)}, u32[]{:S(2)}) async-start(bf16[32,8,1024]{2,0,1:T(8,128)(2,1)} %copy.14), calls=%async_computation.1 | async-start | bytes 1048576 | tf_op jit(solution)/shard_map/all_to_all | solution.py:83
  20.5 12.5 %all-to-all-done.1 = bf16[32,8,1024]{2,0,1:T(8,128)(2,1)S(1)} async-done(((bf16[32,8,1024]{2,0,1:T(8,128)(2,1)}), bf16[32,8,1024]{2,0,1:T(8,128)(2,1)S(1)}, u32[]{:S(2)}, u32[]{:S(2)}) %all-to-all-start.1) | async-done | bytes 524320 | tf_op jit(solution)/shard_map/all_to_all | solution.py:83
  33.0 8.8 %while.21 = (s32[]{:T(128)}, f32[256,256]{1,0:T(8,128)S(1)}, f32[256]{0:T(256)S(1)}, s32[]{:T(128)}, bf16[256,1024]{1,0:T(8,128)(2,1)S(1)}, /*index=5*/s32[]{:T(...) while((s32[]{:T(128)}, f32[256,256]{1,0:T(8,128)S(1)}, ...), condition=%wide.region_3.4_spmd, body=%wide.region_1.3_spmd.sunk | while | flops 101450376 | bytes 798387 | solution.py:50
  33.1 1.4 %compare_select_fusion.2 = (f32[128]{0:T(128)S(1)}, f32[128]{0:T(128)S(1)}) fusion(f32[1024]{0:T(1024)} %get-tuple-element.174, s32[]{:T(128)S(6)} %select_n.27, s32[]{:T(128)} %get-tuple-element.173, s32[]{:T(128)S(6)} %mul.129, f32[128]{0:T(128)S(1)} %convert_reduce_fusion.3), kind=kLoop, calls=%fused_computation.12.clone.1 | loop fusion | flops 512 | bytes 2060 | tf_op jit(solution)/shard_map/while/body/eval_jaxpr/while/body/jit(_where)/select_n | solution.py:20
  34.5 0.5 convolution_add_fusion.3
  35.0 0.9 %fusion.77 = f32[1,256]{1,0:T(1,128)S(1)} fusion(f32[128]{0:T(128)S(1)} %get-tuple-element.142, f32[128]{0:T(128)S(1)} %get-tuple-element.143, bf16[256,1024]{1,0:T(8,128)(2,1)S(1)} %get-tuple-element.172, s32[]{:T(128)S(6)} %select_n.27, f32[1024]{0:T(1024)} %get-tuple-element.175), kind=kOutput, calls=%fused_computation.1.clone.1 | convolution fusion | flops 491520 | bytes 69120 | tf_op jit(solution)/shard_map/while/body/eval_jaxpr/while/body/dot_general | solution.py:23
  36.0 1.4 %compare_select_fusion.2 = (f32[128]{0:T(128)S(1)}, f32[128]{0:T(128)S(1)}) fusion(f32[1024]{0:T(1024)} %get-tuple-element.174, s32[]{:T(128)S(6)} %select_n.27, s32[]{:T(128)} %get-tuple-element.173, s32[]{:T(128)S(6)} %mul.129, f32[128]{0:T(128)S(1)} %convert_reduce_fusion.3), kind=kLoop, calls=%fused_computation.12.clone.1 | loop fusion | flops 512 | bytes 2060 | tf_op jit(solution)/shard_map/while/body/eval_jaxpr/while/body/jit(_where)/select_n | solution.py:20
  37.4 0.5 convolution_add_fusion.3
  37.9 0.9 %fusion.77 = f32[1,256]{1,0:T(1,128)S(1)} fusion(f32[128]{0:T(128)S(1)} %get-tuple-element.142, f32[128]{0:T(128)S(1)} %get-tuple-element.143, bf16[256,1024]{1,0:T(8,128)(2,1)S(1)} %get-tuple-element.172, s32[]{:T(128)S(6)} %select_n.27, f32[1024]{0:T(1024)} %get-tuple-element.175), kind=kOutput, calls=%fused_computation.1.clone.1 | convolution fusion | flops 491520 | bytes 69120 | tf_op jit(solution)/shard_map/while/body/eval_jaxpr/while/body/dot_general | solution.py:23
  38.9 1.4 %compare_select_fusion.2 = (f32[128]{0:T(128)S(1)}, f32[128]{0:T(128)S(1)}) fusion(f32[1024]{0:T(1024)} %get-tuple-element.174, s32[]{:T(128)S(6)} %select_n.27, s32[]{:T(128)} %get-tuple-element.173, s32[]{:T(128)S(6)} %mul.129, f32[128]{0:T(128)S(1)} %convert_reduce_fusion.3), kind=kLoop, calls=%fused_computation.12.clone.1 | loop fusion | flops 512 | bytes 2060 | tf_op jit(solution)/shard_map/while/body/eval_jaxpr/while/body/jit(_where)/select_n | solution.py:20
  40.3 0.5 convolution_add_fusion.3
  40.8 0.9 %fusion.77 = f32[1,256]{1,0:T(1,128)S(1)} fusion(f32[128]{0:T(128)S(1)} %get-tuple-element.142, f32[128]{0:T(128)S(1)} %get-tuple-element.143, bf16[256,1024]{1,0:T(8,128)(2,1)S(1)} %get-tuple-element.172, s32[]{:T(128)S(6)} %select_n.27, f32[1024]{0:T(1024)} %get-tuple-element.175), kind=kOutput, calls=%fused_computation.1.clone.1 | convolution fusion | flops 491520 | bytes 69120 | tf_op jit(solution)/shard_map/while/body/eval_jaxpr/while/body/dot_general | solution.py:23
  41.8 0.7 multiply_reduce_fusion
  43.5 0.4 fusion.26
  47.7 0.4 fusion.13
  49.1 0.7 fusion.19
  49.8 0.5 broadcast.86
  50.3 0.7 reduce.6
  51.0 23.8 %all_to_all.42 = bf16[8,2,4096]{2,1,0:T(2,128)(2,1)S(1)} all-to-all(bf16[8,2,4096]{2,1,0:T(2,128)(2,1)S(1)} %reshape.181), channel_id=1, replica_groups=mesh['mem'=8,'grp'=4] {'mem'}, dimensions={0} | all-to-all | bytes 262144 | tf_op jit(solution)/shard_map/all_to_all | solution.py:87
  75.0 0.7 copy.16
  (29 shorter events, 5.6 us)
Async XLA Ops:
  1.6 14.6 %all-to-all-start = ((bf16[32,8,256]{2,0,1:T(8,128)(2,1)}), bf16[32,8,256]{2,0,1:T(8,128)(2,1)S(1)}, u32[]{:S(2)}, u32[]{:S(2)}) async-start(bf16[32,8,256]{2,0,1:T(8,128)(2,1)} %copy.13), calls=%async_computation | async-start | bytes 262144 | tf_op jit(solution)/shard_map/all_to_all | solution.py:82
  16.2 16.8 %all-to-all-start.1 = ((bf16[32,8,1024]{2,0,1:T(8,128)(2,1)}), bf16[32,8,1024]{2,0,1:T(8,128)(2,1)S(1)}, u32[]{:S(2)}, u32[]{:S(2)}) async-start(bf16[32,8,1024]{2,0,1:T(8,128)(2,1)} %copy.14), calls=%async_computation.1 | async-start | bytes 1048576 | tf_op jit(solution)/shard_map/all_to_all | solution.py:83
where the time goes:
time: 76.3 us; the launch traced here: 75.7 us
  blocking collectives  23.8 us (31%)
  waiting for transfers between devices  17.7 us (23%)
  starting transfers between devices  10.8 us (14%)
  matrix products  10.6 us (14%)
  other arithmetic  5.97 us (8%)
  local copies, waits for them, and re-layouts  5.15 us (7%)
  between operations  1.58 us (2%)
    all_to_all x1, blocking collectives, local(): lax.all_to_all(analysed, 'mem', split_axis=0, concat_axis=1, tiled=True)  23.8 us
    all_to_all x1, waiting for transfers between devices, local(): lax.all_to_all(mapped_prior, 'mem', split_axis=1, concat_axis=0, tiled=True)  12.5 us
    all_to_all x1, starting transfers between devices, local(): lax.all_to_all(prior_members, 'mem', split_axis=1, concat_axis=0, tiled=T...  7.28 us
    all_to_all x1, waiting for transfers between devices, local(): lax.all_to_all(prior_members, 'mem', split_axis=1, concat_axis=0, tiled=T...  5.22 us
    select_n x3, other arithmetic, block_terms(): weights = jnp.where(row_ids < lines_in_play, weight_blk, jnp.float32(0.0))  4.22 us
    unnamed x5, local copies, waits for them, and re-layouts  3.88 us
    all_to_all x1, starting transfers between devices, local(): lax.all_to_all(mapped_prior, 'mem', split_axis=1, concat_axis=0, tiled=True)  3.49 us
    dot_general x3, matrix products, block_terms(): pull_vec = pull_vec + jnp.dot(weighted, innov_blk, precision=highest)  2.71 us
  transfers between devices with their start and end apart: 2, of which 2 were waited for; matrix products, arithmetic and copies ran while one was open for 3% of the time, Pallas kernels for 0%

commit v1 on v0

v1 whole, which is shorter than its diff:
```python
import functools
import math

import jax
import jax.numpy as jnp
from jax import lax
from jax.experimental import pallas as pl
from jax.experimental.pallas import tpu as pltpu
from jax.sharding import PartitionSpec as P

ITERS = 5
BF16 = jnp.bfloat16
F32 = jnp.float32

VMEM = pl.BlockSpec(memory_space=pltpu.VMEM)
SMEM = pl.BlockSpec(memory_space=pltpu.SMEM)


def mm(a, b, contract=(1, 0)):
    dims = (((contract[0],), (contract[1],)), ((), ()))
    return lax.dot_general(a, b, dims, preferred_element_type=F32)


def split(x):
    high = x.astype(BF16)
    return high, (x - high.astype(F32)).astype(BF16)


def mm3(a, b):
    (ah, al), (bh, bl) = split(a), split(b)
    return mm(ah, bh) + (mm(al, bh) + mm(ah, bl))


def analysis_kernel(unknowns, lines_ref, departure_ref, precision_ref, block_ref, out_ref):
    members = block_ref.shape[0]
    state = block_ref[:, :unknowns].astype(F32)
    values = block_ref[:, unknowns:].astype(F32)
    center = jnp.mean(state, axis=0, keepdims=True)
    spread = state - center
    deviat = values - jnp.mean(values, axis=0, keepdims=True)
    row_ids = lax.broadcasted_iota(jnp.int32, precision_ref.shape, 1)
    weights = jnp.where(row_ids < lines_ref[0], precision_ref[...], 0.0)
    root_weights = jnp.sqrt(weights)
    scaled = deviat * root_weights
    half = scaled.astype(BF16)
    gram = mm(half, half, (1, 1))
    pull = jnp.sum(scaled * (root_weights * departure_ref[...]), axis=1, keepdims=True)

    rows = lax.broadcasted_iota(jnp.int32, (members, members), 0)
    columns = lax.broadcasted_iota(jnp.int32, (members, members), 1)
    system = gram + jnp.where(rows == columns, F32(members - 1), 0.0)
    norm2 = jnp.sum(jnp.sum(system * system, axis=0, keepdims=True), axis=1, keepdims=True)
    inv_scale = lax.rsqrt(norm2)
    iterate = system * inv_scale
    eye15 = jnp.where(rows == columns, F32(1.5), 0.0)
    low = iterate.astype(BF16)
    root = eye15 - 0.5 * iterate
    iterate = 1.5 * iterate - 0.5 * mm(low, low)
    for sweep in range(1, ITERS - 1):
        root_low, iterate_low = root.astype(BF16), iterate.astype(BF16)
        product = mm(root_low, iterate_low).astype(BF16)
        iterate = 1.5 * iterate - 0.5 * mm(iterate_low, product)
        root = 1.5 * root - 0.5 * mm(product, root_low)
    product = mm(root.astype(BF16), iterate.astype(BF16))
    right = jnp.concatenate([spread, jnp.broadcast_to(pull, (members, 128))], axis=1)
    right = mm3(root, right)
    right = 1.5 * right - 0.5 * mm3(product, right)
    moved = right[:, :unknowns]
    shift = jnp.sum(moved * right[:, unknowns : unknowns + 1], axis=0, keepdims=True) * inv_scale
    gain = math.sqrt(members - 1) * jnp.sqrt(inv_scale)
    out_ref[...] = (gain * moved + (center + shift)).astype(BF16)


def local(prior_members, mapped_prior, departure, precision_factor, measured_lines, *, devices):
    own, patches, unknowns = prior_members.shape
    rows = mapped_prior.shape[2]
    members = own * devices
    each = patches // devices
    packed = jnp.concatenate([prior_members, mapped_prior], axis=2)
    packed = jnp.transpose(packed, (1, 0, 2))
    packed = lax.all_to_all(packed, "mem", split_axis=0, concat_axis=0, tiled=True)
    packed = packed.reshape(devices, each, own, unknowns + rows)
    kernel = pl.pallas_call(
        functools.partial(analysis_kernel, unknowns),
        out_shape=jax.ShapeDtypeStruct((members, unknowns), BF16),
        in_specs=[SMEM, VMEM, VMEM, VMEM],
        out_specs=VMEM,
        compiler_params=pltpu.CompilerParams(vmem_limit_bytes=16 << 20),
    )
    results = [
        kernel(
            measured_lines[k : k + 1],
            departure[k : k + 1],
            precision_factor[k : k + 1],
            packed[:, k].reshape(members, unknowns + rows),
        )
        for k in range(each)
    ]
    analysed = jnp.stack([r.reshape(devices, own, unknowns) for r in results], axis=1)
    analysed = analysed.reshape(patches, own, unknowns)
    analysed = lax.all_to_all(analysed, "mem", split_axis=0, concat_axis=0, tiled=True)
    return jnp.transpose(analysed, (1, 0, 2))


def solution(mesh):
    in_specs = (
        P("mem", "grp", None),
        P("mem", "grp", None),
        P(("grp", "mem"), None),
        P(("grp", "mem"), None),
        P(("grp", "mem")),
    )
    body = functools.partial(local, devices=mesh.shape["mem"])
    return jax.shard_map(
        body, mesh=mesh, in_specs=in_specs, out_specs=P("mem", "grp", None), check_vma=False
    )
```

time: 76.3 us -> 41.6 us (0.55)
  blocking collectives: 23.8 us -> 10.8 us
  matrix products: 10.6 us -> 0 us
  other arithmetic: 5.97 us -> 0.9 us
  starting transfers between devices: 10.8 us -> 7.41 us
  local copies, waits for them, and re-layouts: 5.15 us -> 2.14 us
  Pallas kernels: 0 us -> 2.76 us
  waiting for transfers between devices: 17.7 us -> 16.6 us
  between operations: 1.58 us -> 0.68 us
    all_to_all x1, blocking collectives: 23.8 us -> 10.8 us  [local(): lax.all_to_all(analysed, 'mem', split_axis=0, concat_axis=0, tiled=True)]
    dot_general x23 -> x0, matrix products: 10.6 us -> none  [the longest x3 2.71 us: block_terms(): pull_vec = pull_vec + jnp.dot(weighted, innov_blk, precision=highest)]
    select_n x3 -> x0, other arithmetic: 4.22 us -> none  [block_terms(): weights = jnp.where(row_ids < lines_in_play, weight_blk, jnp.float32(0.0))]
    all_to_all x2 -> x1, starting transfers between devices: 10.8 us -> 7.41 us  [local(): lax.all_to_all(packed, 'mem', split_axis=0, concat_axis=0, tiled=True)]
    pallas_call x0 -> x1, Pallas kernels: none -> 2.76 us  [local(): kernel(measured_lines[k:k + 1], departure[k:k + 1], precision_factor[k:k...]
    unnamed x5 -> x8, local copies, waits for them, and re-layouts: 3.88 us -> 1.41 us
    all_to_all x2 -> x1, waiting for transfers between devices: 17.7 us -> 16.6 us  [local(): lax.all_to_all(packed, 'mem', split_axis=0, concat_axis=0, tiled=True)]
    transpose x0 -> x1, other arithmetic: none -> 0.9 us  [local(): packed = jnp.transpose(packed, (1, 0, 2))]
  transfers between devices with their start and end apart: 2 -> 1, of which waited for: 2 -> 1; matrix products, arithmetic and copies ran while one was open for 3% -> 0% of each run, Pallas kernels for 0% -> 0%
where the time goes in v1:
time: 41.6 us; the launch traced here: 41.3 us
  waiting for transfers between devices  16.6 us (40%)
  blocking collectives  10.8 us (26%)
  starting transfers between devices  7.41 us (18%)
  Pallas kernels  2.76 us (7%)
  local copies, waits for them, and re-layouts  2.14 us (5%)
  other arithmetic  0.9 us (2%)
  between operations  0.68 us (2%)
    all_to_all x1, waiting for transfers between devices, local(): lax.all_to_all(packed, 'mem', split_axis=0, concat_axis=0, tiled=True)  16.6 us
    all_to_all x1, blocking collectives, local(): lax.all_to_all(analysed, 'mem', split_axis=0, concat_axis=0, tiled=True)  10.8 us
    all_to_all x1, starting transfers between devices, local(): lax.all_to_all(packed, 'mem', split_axis=0, concat_axis=0, tiled=True)  7.41 us
    pallas_call x1, Pallas kernels, local(): kernel(measured_lines[k:k + 1], departure[k:k + 1], precision_factor[k:k...  2.76 us
    unnamed x8, local copies, waits for them, and re-layouts  1.41 us
    transpose x1, other arithmetic, local(): packed = jnp.transpose(packed, (1, 0, 2))  0.9 us
  transfers between devices with their start and end apart: 1, of which 1 were waited for; matrix products, arithmetic and copies ran while one was open for 0% of the time, Pallas kernels for 0%

profile of v1, /device:TPU:0, one launch (start us, length us, event | category | flops | bytes accessed | tf_op | source)
XLA Modules:
  0.0 41.3 jit_solution(14080350949019356837)
XLA Ops:
  0.0 0.0 copy-start.2
  0.0 1.4 %copy.9 = bf16[32,8,1024]{2,0,1:T(8,128)(2,1)S(1)} copy(bf16[32,8,1024]{2,1,0:T(8,128)(2,1)} %param.6) | data formatting | bytes 1048576 | tf_op args[1]
  1.4 0.0 copy-done.2
  1.4 0.9 %maximum_bitcast_fusion = bf16[8,32,1280]{2,1,0:T(8,128)(2,1)} fusion(bf16[32,8,1024]{2,0,1:T(8,128)(2,1)S(1)} %copy.9, bf16[32,8,256]{2,0,1:T(8,128)(2,1)S(1)} %copy.8), kind=kLoop, calls=%fused_computation | loop fusion | flops 1310720 | bytes 1310720 | tf_op jit(solution)/shard_map/transpose | solution.py:80
  2.3 0.0 copy-start
  2.3 0.0 copy-start.1
  2.3 7.4 %all-to-all-start = ((bf16[8,32,1280]{2,1,0:T(8,128)(2,1)}), bf16[8,32,1280]{2,1,0:T(8,128)(2,1)S(1)}, u32[]{:S(2)}, u32[]{:S(2)}) async-start(bf16[8,32,1280]{2,1,0:T(8,128)(2,1)} %maximum_bitcast_fusion), calls=%async_computation | async-start | bytes 1310720 | tf_op jit(solution)/shard_map/all_to_all | solution.py:81
  10.4 16.6 %all-to-all-done = bf16[8,32,1280]{2,1,0:T(8,128)(2,1)S(1)} async-done(((bf16[8,32,1280]{2,1,0:T(8,128)(2,1)}), bf16[8,32,1280]{2,1,0:T(8,128)(2,1)S(1)}, u32[]{:S(2)}, u32[]{:S(2)}) %all-to-all-start) | async-done | bytes 655392 | tf_op jit(solution)/shard_map/all_to_all | solution.py:81
  27.0 0.0 copy-done
  27.0 0.0 copy-done.1
  27.0 2.8 %shard_map.55 = bf16[256,256]{1,0:T(8,128)(2,1)S(1)} custom-call(s32[1]{0:T(128)S(6)} %copy.11.lines_ref, f32[1,1024]{1,0:T(1,128)S(1)} %copy-done, f32[1,1024]{1,0:T(1,128)S(1)} %copy-done.1, bf16[256,1280]{1,0:T(8,128)(2,1)S(1)} %bitcast.5), custom_call_target="tpu_custom_call" | custom-call | tf_op jit(solution)/shard_map/pallas_call | solution.py:91
  29.8 10.8 %all_to_all.10 = bf16[8,32,256]{2,1,0:T(8,128)(2,1)S(1)} all-to-all(bf16[8,32,256]{2,1,0:T(8,128)(2,1)S(1)} %bitcast.6), channel_id=1, replica_groups=mesh['mem'=8,'grp'=4] {'mem'}, dimensions={0} | all-to-all | bytes 262144 | tf_op jit(solution)/shard_map/all_to_all | solution.py:101
  40.6 0.7 %copy.10 = bf16[32,8,256]{2,1,0:T(8,128)(2,1)} copy(bf16[32,8,256]{2,0,1:T(8,128)(2,1)S(1)} %bitcast.7) | data formatting | bytes 262144 | tf_op jit(solution)/shard_map/transpose | solution.py:102
  (1 shorter events, 0.0 us)
Async XLA Ops:
  0.0 1.4 %copy-start.2 = (bf16[32,8,256]{2,1,0:T(8,128)(2,1)S(1)}, bf16[32,8,256]{2,1,0:T(8,128)(2,1)}, u32[]{:S(2)}) copy-start(bf16[32,8,256]{2,1,0:T(8,128)(2,1)} %param.5) | copy-start | bytes 393220
  2.3 24.7 %copy-start = (f32[1,1024]{1,0:T(1,128)S(1)}, f32[1,1024]{1,0:T(1,128)}, u32[]{:S(2)}) copy-start(f32[1,1024]{1,0:T(1,128)} %departure_ref.1) | copy-start | bytes 12292
  2.3 24.7 %copy-start.1 = (f32[1,1024]{1,0:T(1,128)S(1)}, f32[1,1024]{1,0:T(1,128)}, u32[]{:S(2)}) copy-start(f32[1,1024]{1,0:T(1,128)} %precision_ref.1) | copy-start | bytes 12292
  2.3 24.7 %all-to-all-start = ((bf16[8,32,1280]{2,1,0:T(8,128)(2,1)}), bf16[8,32,1280]{2,1,0:T(8,128)(2,1)S(1)}, u32[]{:S(2)}, u32[]{:S(2)}) async-start(bf16[8,32,1280]{2,1,0:T(8,128)(2,1)} %maximum_bitcast_fusion), calls=%async_computation | async-start | bytes 1310720 | tf_op jit(solution)/shard_map/all_to_all | solution.py:81

commit v2 on v1

v2 whole, which is shorter than its diff:
```python
import functools
import math

import jax
import jax.numpy as jnp
from jax import lax
from jax.experimental import pallas as pl
from jax.experimental.pallas import tpu as pltpu
from jax.sharding import PartitionSpec as P


ITERS = 5
PAIRWISE_LIMIT = 16
BF16 = jnp.bfloat16
F32 = jnp.float32

VMEM = pl.BlockSpec(memory_space=pltpu.VMEM)
SMEM = pl.BlockSpec(memory_space=pltpu.SMEM)
HBM = pl.BlockSpec(memory_space=pltpu.HBM)
PARAMS = pltpu.CompilerParams(vmem_limit_bytes=16 << 20)


def mm(a, b, contract=(1, 0)):
    dims = (((contract[0],), (contract[1],)), ((), ()))
    return lax.dot_general(a, b, dims, preferred_element_type=F32)


def split(x):
    high = x.astype(BF16)
    return high, (x - high.astype(F32)).astype(BF16)


def mm3(a, b):
    (ah, al), (bh, bl) = split(a), split(b)
    return mm(ah, bh) + (mm(al, bh) + mm(ah, bl))


def pack_kernel(me_ref, prior_ref, mapped_ref, *refs):
    own, patches, unknowns = prior_ref.shape
    out_refs, (prior_vmem, mapped_vmem, sems) = refs[:-3], refs[-3:]
    mapped_copy = pltpu.make_async_copy(mapped_ref, mapped_vmem, sems.at[0])
    prior_copy = pltpu.make_async_copy(prior_ref, prior_vmem, sems.at[1])
    mapped_copy.start()
    prior_copy.start()
    size = own * patches
    row = lax.broadcasted_iota(jnp.int32, (size, size), 0)
    column = lax.broadcasted_iota(jnp.int32, (size, size), 1)
    target = (row % own) * patches + ((row // own) ^ me_ref[0])
    pick = jnp.where(column == target, F32(1), F32(0)).astype(BF16)
    for source, place, copy in ((mapped_vmem, unknowns, mapped_copy), (prior_vmem, 0, prior_copy)):
        width = source.shape[2]
        copy.wait()
        moved = mm(pick, source[...].reshape(size, width)).astype(BF16)
        for s, out_ref in enumerate(out_refs):
            out_ref[:, place : place + width] = moved[s * own : (s + 1) * own]


def analysis_kernel(unknowns, me_ref, lines_ref, departure_ref, precision_ref, *refs):
    block_refs, out_ref = refs[:-1], refs[-1]
    block = jnp.concatenate([r[...] for r in block_refs], axis=0)
    members = block.shape[0]
    state = block[:, :unknowns].astype(F32)
    values = block[:, unknowns:].astype(F32)
    center = jnp.mean(state, axis=0, keepdims=True)
    spread = state - center
    deviat = values - jnp.mean(values, axis=0, keepdims=True)
    row_ids = lax.broadcasted_iota(jnp.int32, precision_ref.shape, 1)
    weights = jnp.where(row_ids < lines_ref[0], precision_ref[...], 0.0)
    root_weights = jnp.sqrt(weights)
    scaled = deviat * root_weights
    half = scaled.astype(BF16)
    gram = mm(half, half, (1, 1))
    pull = jnp.sum(scaled * (root_weights * departure_ref[...]), axis=1, keepdims=True)

    rows = lax.broadcasted_iota(jnp.int32, (members, members), 0)
    columns = lax.broadcasted_iota(jnp.int32, (members, members), 1)
    system = gram + jnp.where(rows == columns, F32(members - 1), 0.0)
    norm2 = jnp.sum(jnp.sum(system * system, axis=0, keepdims=True), axis=1, keepdims=True)
    inv_scale = lax.rsqrt(norm2)
    iterate = system * inv_scale
    low = iterate.astype(BF16)
    root = jnp.where(rows == columns, F32(1.5), 0.0) - 0.5 * iterate
    iterate = 1.5 * iterate - 0.5 * mm(low, low)
    for _ in range(1, ITERS - 1):
        root_low, iterate_low = root.astype(BF16), iterate.astype(BF16)
        product = mm(root_low, iterate_low).astype(BF16)
        iterate = 1.5 * iterate - 0.5 * mm(iterate_low, product)
        root = 1.5 * root - 0.5 * mm(product, root_low)
    product = mm(root.astype(BF16), iterate.astype(BF16))
    right = jnp.concatenate([spread, jnp.broadcast_to(pull, (members, 128))], axis=1)
    right = mm3(root, right)
    right = 1.5 * right - 0.5 * mm3(product, right)
    moved = right[:, :unknowns]
    shift = jnp.sum(moved * right[:, unknowns : unknowns + 1], axis=0, keepdims=True) * inv_scale
    gain = math.sqrt(members - 1) * jnp.sqrt(inv_scale)
    result = (gain * moved + (center + shift)).astype(BF16)
    if len(block_refs) == 1:
        out_ref[...] = result
    else:
        own = members // len(block_refs)
        for s in range(len(block_refs)):
            out_ref[me_ref[0] ^ s] = result[s * own : (s + 1) * own]


def analyse(me, lines, departure, precision, blocks, unknowns):
    members = sum(b.shape[0] for b in blocks)
    shape = (members, unknowns)
    if len(blocks) > 1:
        shape = (len(blocks), members // len(blocks), unknowns)
    return pl.pallas_call(
        functools.partial(analysis_kernel, unknowns),
        out_shape=jax.ShapeDtypeStruct(shape, BF16),
        in_specs=[SMEM, SMEM, VMEM, VMEM] + [VMEM] * len(blocks),
        out_specs=VMEM,
        compiler_params=PARAMS,
    )(me, lines, departure, precision, *blocks)


def local_pairs(prior_members, mapped_prior, departure, precision_factor, measured_lines, *, devices):
    own, _, unknowns = prior_members.shape
    width = unknowns + mapped_prior.shape[2]
    me = lax.axis_index("mem").astype(jnp.int32).reshape(1)
    blocks = pl.pallas_call(
        pack_kernel,
        out_shape=[jax.ShapeDtypeStruct((own, width), BF16)] * devices,
        in_specs=[SMEM, HBM, HBM],
        out_specs=[VMEM] * devices,
        scratch_shapes=[
            pltpu.VMEM(prior_members.shape, BF16),
            pltpu.VMEM(mapped_prior.shape, BF16),
            pltpu.SemaphoreType.DMA((2,)),
        ],
        compiler_params=PARAMS,
    )(
        me,
        pltpu.with_memory_space_constraint(prior_members, pltpu.HBM),
        pltpu.with_memory_space_constraint(mapped_prior, pltpu.HBM),
    )
    arrived = [blocks[0]]
    for s in range(1, devices):
        pairs = [(a, a ^ s) for a in range(devices)]
        arrived.append(lax.ppermute(blocks[s], "mem", pairs))
    result = analyse(me, measured_lines, departure, precision_factor, arrived, unknowns)
    result = lax.all_to_all(result, "mem", split_axis=0, concat_axis=0, tiled=True)
    return jnp.transpose(result, (1, 0, 2))


def local_any(prior_members, mapped_prior, departure, precision_factor, measured_lines, *, devices):
    own, patches, unknowns = prior_members.shape
    rows = mapped_prior.shape[2]
    each = patches // devices
    packed = jnp.concatenate([prior_members, mapped_prior], axis=2)
    packed = jnp.transpose(packed, (1, 0, 2))
    packed = lax.all_to_all(packed, "mem", split_axis=0, concat_axis=0, tiled=True)
    packed = packed.reshape(devices, each, own, unknowns + rows)
    me = jnp.zeros((1,), jnp.int32)
    results = []
    for k in range(each):
        at = slice(k, k + 1)
        block = packed[:, k].reshape(devices * own, unknowns + rows)
        result = analyse(
            me, measured_lines[at], departure[at], precision_factor[at], [block], unknowns
        )
        results.append(result.reshape(devices, own, unknowns))
    result = jnp.stack(results, axis=1).reshape(patches, own, unknowns)
    result = lax.all_to_all(result, "mem", split_axis=0, concat_axis=0, tiled=True)
    return jnp.transpose(result, (1, 0, 2))


def solution(mesh):
    devices = mesh.shape["mem"]
    in_specs = (
        P("mem", "grp", None),
        P("mem", "grp", None),
        P(("grp", "mem"), None),
        P(("grp", "mem"), None),
        P(("grp", "mem")),
    )

    def step(prior_members, mapped_prior, departure, precision_factor, measured_lines):
        each = departure.shape[0] // mesh.size
        pairwise = each == 1 and devices <= PAIRWISE_LIMIT and devices & (devices - 1) == 0
        body = functools.partial(local_pairs if pairwise else local_any, devices=devices)
        return jax.shard_map(
            body, mesh=mesh, in_specs=in_specs, out_specs=P("mem", "grp", None), check_vma=False
        )(prior_members, mapped_prior, departure, precision_factor, measured_lines)

    return step
```

time: 41.6 us -> 38.9 us (0.935)
  waiting for transfers between devices: 16.6 us -> 7.66 us
  starting transfers between devices: 7.41 us -> 12.5 us
  blocking collectives: 10.8 us -> 12.7 us
  Pallas kernels: 2.76 us -> 4.4 us
  local copies, waits for them, and re-layouts: 2.14 us -> 0.74 us
  other arithmetic: 0.9 us -> 0 us
    all_to_all x1 -> x0, waiting for transfers between devices: 16.6 us -> none  [local(): lax.all_to_all(packed, 'mem', split_axis=0, concat_axis=0, tiled=True)]
    ppermute x0 -> x7, starting transfers between devices: none -> 12.5 us  [local_pairs(): arrived.append(lax.ppermute(blocks[s], 'mem', pairs))]
    ppermute x0 -> x7, waiting for transfers between devices: none -> 7.66 us  [local_pairs(): arrived.append(lax.ppermute(blocks[s], 'mem', pairs))]
    all_to_all x1 -> x0, starting transfers between devices: 7.41 us -> none  [local(): lax.all_to_all(packed, 'mem', split_axis=0, concat_axis=0, tiled=True)]
    all_to_all x1, blocking collectives: 10.8 us -> 12.7 us  [local_pairs(): lax.all_to_all(result, 'mem', split_axis=0, concat_axis=0, tiled=True)]
    pallas_call x1 -> x2, Pallas kernels: 2.76 us -> 4.4 us  [the longest x1 2.78 us: analyse(): pl.pallas_call(functools.partial(analysis_kernel, unknowns), out_shape=ja...]
    unnamed x8 -> x4, local copies, waits for them, and re-layouts: 1.41 us -> 0.01 us
    transpose x1 -> x0, other arithmetic: 0.9 us -> none  [local(): packed = jnp.transpose(packed, (1, 0, 2))]
  transfers between devices with their start and end apart: 1 -> 7, of which waited for: 1 -> 1; matrix products, arithmetic and copies ran while one was open for 0% -> 0% of each run, Pallas kernels for 0% -> 0%
where the time goes in v2:
time: 38.9 us; the launch traced here: 38.7 us
  blocking collectives  12.7 us (33%)
  starting transfers between devices  12.5 us (32%)
  waiting for transfers between devices  7.66 us (20%)
  Pallas kernels  4.4 us (11%)
  local copies, waits for them, and re-layouts  0.74 us (2%)
  between operations  0.7 us (2%)
    all_to_all x1, blocking collectives, local_pairs(): lax.all_to_all(result, 'mem', split_axis=0, concat_axis=0, tiled=True)  12.7 us
    ppermute x7, starting transfers between devices, local_pairs(): arrived.append(lax.ppermute(blocks[s], 'mem', pairs))  12.5 us
    ppermute x7, waiting for transfers between devices, local_pairs(): arrived.append(lax.ppermute(blocks[s], 'mem', pairs))  7.66 us
    pallas_call x1, Pallas kernels, analyse(): pl.pallas_call(functools.partial(analysis_kernel, unknowns), out_shape=ja...  2.78 us
    pallas_call x1, Pallas kernels, local_pairs(): pl.pallas_call(pack_kernel, out_shape=[jax.ShapeDtypeStruct((own, width),...  1.61 us
  transfers between devices with their start and end apart: 7, of which 1 were waited for; matrix products, arithmetic and copies ran while one was open for 0% of the time, Pallas kernels for 0%

profile of v2, /device:TPU:0, one launch (start us, length us, event | category | flops | bytes accessed | tf_op | source)
XLA Modules:
  0.0 38.7 jit_solution(4176547899119642278)
XLA Ops:
  0.0 1.6 %shard_map.55 = (bf16[32,1280]{1,0:T(8,128)(2,1)S(1)}, bf16[32,1280]{1,0:T(8,128)(2,1)S(1)}, bf16[32,1280]{1,0:T(8,128)(2,1)S(1)}, bf16[32,1280]{1,0:T(8,128)(2,...) custom-call(s32[1]{0:T(128)} %bitcast.me_ref, ...), custom_call_target="tpu_custom_call" | custom-call | tf_op jit(solution)/shard_map/pallas_call | solution.py:123
  1.6 3.0 %collective-permute-start = (bf16[32,1280]{1,0:T(8,128)(2,1)S(1)}, bf16[32,1280]{1,0:T(8,128)(2,1)S(1)}, u32[]{:S(2)}, u32[]{:S(2)}) collective-permute-start(bf16[32,1280]{1,0:T(8,128)(2,1)S(1)} %get-tuple-element.14), channel_id=1, source_target_pairs={{0,4},{4,0},{8,12},{12,8},{16,20},{20,16},{24,28},{28,24},{1,5},{5... | collective-permute-start | bytes 245768 | tf_op jit(solution)/shard_map/ppermute | solution.py:142
  4.7 1.6 %collective-permute-start.1 = (bf16[32,1280]{1,0:T(8,128)(2,1)S(1)}, bf16[32,1280]{1,0:T(8,128)(2,1)S(1)}, u32[]{:S(2)}, u32[]{:S(2)}) collective-permute-start(bf16[32,1280]{1,0:T(8,128)(2,1)S(1)} %get-tuple-element.15), channel_id=1, source_target_pairs={{0,8},{4,12},{8,0},{12,4},{16,24},{20,28},{24,16},{28,20},{1,9},{5... | collective-permute-start | bytes 245768 | tf_op jit(solution)/shard_map/ppermute | solution.py:142
  6.2 0.0 collective-permute-start.2
  6.2 3.0 %collective-permute-start.3 = (bf16[32,1280]{1,0:T(8,128)(2,1)S(1)}, bf16[32,1280]{1,0:T(8,128)(2,1)S(1)}, u32[]{:S(2)}, u32[]{:S(2)}) collective-permute-start(bf16[32,1280]{1,0:T(8,128)(2,1)S(1)} %get-tuple-element.17), channel_id=1, source_target_pairs={{0,16},{4,20},{8,24},{12,28},{16,0},{20,4},{24,8},{28,12},{1,17},{... | collective-permute-start | bytes 245768 | tf_op jit(solution)/shard_map/ppermute | solution.py:142
  9.2 0.0 copy-start.1
  9.2 0.0 copy-start
  9.2 1.3 %collective-permute-start.4 = (bf16[32,1280]{1,0:T(8,128)(2,1)S(1)}, bf16[32,1280]{1,0:T(8,128)(2,1)S(1)}, u32[]{:S(2)}, u32[]{:S(2)}) collective-permute-start(bf16[32,1280]{1,0:T(8,128)(2,1)S(1)} %get-tuple-element.18), channel_id=1, source_target_pairs={{0,20},{4,16},{8,28},{12,24},{16,4},{20,0},{24,12},{28,8},{1,21},{... | collective-permute-start | bytes 245768 | tf_op jit(solution)/shard_map/ppermute | solution.py:142
  10.5 0.0 collective-permute-done.refs_1_
  10.5 3.6 %collective-permute-start.5 = (bf16[32,1280]{1,0:T(8,128)(2,1)S(1)}, bf16[32,1280]{1,0:T(8,128)(2,1)S(1)}, u32[]{:S(2)}, u32[]{:S(2)}) collective-permute-start(bf16[32,1280]{1,0:T(8,128)(2,1)S(1)} %get-tuple-element.19), channel_id=1, source_target_pairs={{0,24},{4,28},{8,16},{12,20},{16,8},{20,12},{24,0},{28,4},{1,25},{... | collective-permute-start | bytes 245768 | tf_op jit(solution)/shard_map/ppermute | solution.py:142
  14.1 0.0 collective-permute-done.1.refs_2_
  14.1 0.0 collective-permute-start.6
  14.8 0.0 collective-permute-done.2.refs_3_
  14.8 0.0 collective-permute-done.3.refs_4_
  14.8 7.6 %collective-permute-done.4.refs_5_ = bf16[32,1280]{1,0:T(8,128)(2,1)S(1)} collective-permute-done((bf16[32,1280]{1,0:T(8,128)(2,1)S(1)}, bf16[32,1280]{1,0:T(8,128)(2,1)S(1)}, u32[]{:S(2)}, u32[]{:S(2)}) %collective-permute-start.4) | collective-permute-done | bytes 81952 | tf_op jit(solution)/shard_map/ppermute | solution.py:142
  22.5 0.0 collective-permute-done.5.refs_6_
  22.5 0.0 collective-permute-done.6.refs_7_
  22.5 0.0 copy-done.1
  22.5 0.0 copy-done
  22.5 2.8 %shard_map.56 = bf16[8,32,256]{2,1,0:T(8,128)(2,1)S(1)} custom-call(s32[1]{0:T(128)} %bitcast.me_ref, s32[1]{0:T(128)S(6)} %copy.7.lines_ref, f32[1,1024]{1,0:T(1,128)S(1)} %copy-done, f32[1,1024]{1,0:T(1,128)S(1)} %copy-done.1, bf16[32,1280]{1,0:T(8,128)(2,1)S(1)} %get-tuple-element.13.refs_0_, bf16[32,1280]{1,0:T(8,128)(2,1)S(1)} %collective-permute-done.refs_1_, ...), custom_call_target="tpu_custom_call" | custom-call | tf_op jit(solution)/shard_map/pallas_call | solution.py:110
  25.3 12.7 %all_to_all.5 = bf16[8,32,256]{2,1,0:T(8,128)(2,1)S(1)} all-to-all(bf16[8,32,256]{2,1,0:T(8,128)(2,1)S(1)} %shard_map.56), channel_id=1, replica_groups=mesh['mem'=8,'grp'=4] {'mem'}, dimensions={0} | all-to-all | bytes 262144 | tf_op jit(solution)/shard_map/all_to_all | solution.py:144
  38.0 0.7 %copy.6 = bf16[32,8,256]{2,1,0:T(8,128)(2,1)} copy(bf16[32,8,256]{2,0,1:T(8,128)(2,1)S(1)} %bitcast.2) | data formatting | bytes 262144 | tf_op jit(solution)/shard_map/transpose | solution.py:145
Async XLA Ops:
  1.6 8.9 %collective-permute-start = (bf16[32,1280]{1,0:T(8,128)(2,1)S(1)}, bf16[32,1280]{1,0:T(8,128)(2,1)S(1)}, u32[]{:S(2)}, u32[]{:S(2)}) collective-permute-start(bf16[32,1280]{1,0:T(8,128)(2,1)S(1)} %get-tuple-element.14), channel_id=1, source_target_pairs={{0,4},{4,0},{8,12},{12,8},{16,20},{20,16},{24,28},{28,24},{1,5},{5... | collective-permute-start | bytes 245768 | tf_op jit(solution)/shard_map/ppermute | solution.py:142
  4.7 9.5 %collective-permute-start.1 = (bf16[32,1280]{1,0:T(8,128)(2,1)S(1)}, bf16[32,1280]{1,0:T(8,128)(2,1)S(1)}, u32[]{:S(2)}, u32[]{:S(2)}) collective-permute-start(bf16[32,1280]{1,0:T(8,128)(2,1)S(1)} %get-tuple-element.15), channel_id=1, source_target_pairs={{0,8},{4,12},{8,0},{12,4},{16,24},{20,28},{24,16},{28,20},{1,9},{5... | collective-permute-start | bytes 245768 | tf_op jit(solution)/shard_map/ppermute | solution.py:142
  6.2 8.6 %collective-permute-start.2 = (bf16[32,1280]{1,0:T(8,128)(2,1)S(1)}, bf16[32,1280]{1,0:T(8,128)(2,1)S(1)}, u32[]{:S(2)}, u32[]{:S(2)}) collective-permute-start(bf16[32,1280]{1,0:T(8,128)(2,1)S(1)} %get-tuple-element.16), channel_id=1, source_target_pairs={{0,12},{4,8},{8,4},{12,0},{16,28},{20,24},{24,20},{28,16},{1,13},{... | collective-permute-start | bytes 245768 | tf_op jit(solution)/shard_map/ppermute | solution.py:142
  6.2 8.6 %collective-permute-start.3 = (bf16[32,1280]{1,0:T(8,128)(2,1)S(1)}, bf16[32,1280]{1,0:T(8,128)(2,1)S(1)}, u32[]{:S(2)}, u32[]{:S(2)}) collective-permute-start(bf16[32,1280]{1,0:T(8,128)(2,1)S(1)} %get-tuple-element.17), channel_id=1, source_target_pairs={{0,16},{4,20},{8,24},{12,28},{16,0},{20,4},{24,8},{28,12},{1,17},{... | collective-permute-start | bytes 245768 | tf_op jit(solution)/shard_map/ppermute | solution.py:142
  9.2 13.2 %copy-start.1 = (f32[1,1024]{1,0:T(1,128)S(1)}, f32[1,1024]{1,0:T(1,128)}, u32[]{:S(2)}) copy-start(f32[1,1024]{1,0:T(1,128)} %precision_ref.1) | copy-start | bytes 12292
  9.2 13.2 %copy-start = (f32[1,1024]{1,0:T(1,128)S(1)}, f32[1,1024]{1,0:T(1,128)}, u32[]{:S(2)}) copy-start(f32[1,1024]{1,0:T(1,128)} %departure_ref.1) | copy-start | bytes 12292
  9.2 13.2 %collective-permute-start.4 = (bf16[32,1280]{1,0:T(8,128)(2,1)S(1)}, bf16[32,1280]{1,0:T(8,128)(2,1)S(1)}, u32[]{:S(2)}, u32[]{:S(2)}) collective-permute-start(bf16[32,1280]{1,0:T(8,128)(2,1)S(1)} %get-tuple-element.18), channel_id=1, source_target_pairs={{0,20},{4,16},{8,28},{12,24},{16,4},{20,0},{24,12},{28,8},{1,21},{... | collective-permute-start | bytes 245768 | tf_op jit(solution)/shard_map/ppermute | solution.py:142
  10.5 12.0 %collective-permute-start.5 = (bf16[32,1280]{1,0:T(8,128)(2,1)S(1)}, bf16[32,1280]{1,0:T(8,128)(2,1)S(1)}, u32[]{:S(2)}, u32[]{:S(2)}) collective-permute-start(bf16[32,1280]{1,0:T(8,128)(2,1)S(1)} %get-tuple-element.19), channel_id=1, source_target_pairs={{0,24},{4,28},{8,16},{12,20},{16,8},{20,12},{24,0},{28,4},{1,25},{... | collective-permute-start | bytes 245768 | tf_op jit(solution)/shard_map/ppermute | solution.py:142
  14.1 8.4 %collective-permute-start.6 = (bf16[32,1280]{1,0:T(8,128)(2,1)S(1)}, bf16[32,1280]{1,0:T(8,128)(2,1)S(1)}, u32[]{:S(2)}, u32[]{:S(2)}) collective-permute-start(bf16[32,1280]{1,0:T(8,128)(2,1)S(1)} %get-tuple-element.20), channel_id=1, source_target_pairs={{0,28},{4,24},{8,20},{12,16},{16,12},{20,8},{24,4},{28,0},{1,29},{... | collective-permute-start | bytes 245768 | tf_op jit(solution)/shard_map/ppermute | solution.py:142

commit v3 on v2

--- a/solution.py
+++ b/solution.py
@@ -11,6 +11,15 @@
 
 ITERS = 5
 PAIRWISE_LIMIT = 16
+ROUNDS = (
+    (6, 7, 4, 5, 2, 3, 0, 1),
+    (5, 4, 6, 7, 1, 0, 2, 3),
+    (3, 6, 7, 0, 5, 4, 1, 2),
+    (7, 3, 5, 1, 6, 2, 4, 0),
+    (4, 2, 1, 6, 0, 7, 3, 5),
+    (1, 0, 3, 2, 7, 6, 5, 4),
+    (2, 5, 0, 4, 3, 1, 7, 6),
+)
 BF16 = jnp.bfloat16
 F32 = jnp.float32
 
@@ -33,6 +42,19 @@
 def mm3(a, b):
     (ah, al), (bh, bl) = split(a), split(b)
     return mm(ah, bh) + (mm(al, bh) + mm(ah, bl))
+
+
+def partner_of(partners, me):
+    found = jnp.int32(partners[0])
+    for d in range(1, len(partners)):
+        found = jnp.where(me == d, jnp.int32(partners[d]), found)
+    return found
+
+
+def rounds_of(devices):
+    if devices == len(ROUNDS) + 1:
+        return ROUNDS
+    return [[a ^ k for a in range(devices)] for k in range(devices - 1, 0, -1)]
 
 
 def pack_kernel(me_ref, prior_ref, mapped_ref, *refs):
@@ -45,7 +67,11 @@
     size = own * patches
     row = lax.broadcasted_iota(jnp.int32, (size, size), 0)
     column = lax.broadcasted_iota(jnp.int32, (size, size), 1)
-    target = (row % own) * patches + ((row // own) ^ me_ref[0])
+    block = row // own
+    patch = jnp.full(row.shape, me_ref[0])
+    for k, partners in enumerate(rounds_of(patches)):
+        patch = jnp.where(block == k + 1, partner_of(partners, me_ref[0]), patch)
+    target = (row % own) * patches + patch
     pick = jnp.where(column == target, F32(1), F32(0)).astype(BF16)
     for source, place, copy in ((mapped_vmem, unknowns, mapped_copy), (prior_vmem, 0, prior_copy)):
         width = source.shape[2]
@@ -74,32 +100,39 @@
 
     rows = lax.broadcasted_iota(jnp.int32, (members, members), 0)
     columns = lax.broadcasted_iota(jnp.int32, (members, members), 1)
+
+    def to_column(row):
+        return jnp.sum(jnp.where(rows == columns, row, 0.0), axis=1, keepdims=True)
+
     system = gram + jnp.where(rows == columns, F32(members - 1), 0.0)
     norm2 = jnp.sum(jnp.sum(system * system, axis=0, keepdims=True), axis=1, keepdims=True)
     inv_scale = lax.rsqrt(norm2)
     iterate = system * inv_scale
-    low = iterate.astype(BF16)
+    low = system.astype(BF16)
+    square = mm(low, low) * (inv_scale * inv_scale)
     root = jnp.where(rows == columns, F32(1.5), 0.0) - 0.5 * iterate
-    iterate = 1.5 * iterate - 0.5 * mm(low, low)
+    iterate = 1.5 * iterate - 0.5 * square
     for _ in range(1, ITERS - 1):
         root_low, iterate_low = root.astype(BF16), iterate.astype(BF16)
         product = mm(root_low, iterate_low).astype(BF16)
         iterate = 1.5 * iterate - 0.5 * mm(iterate_low, product)
         root = 1.5 * root - 0.5 * mm(product, root_low)
     product = mm(root.astype(BF16), iterate.astype(BF16))
-    right = jnp.concatenate([spread, jnp.broadcast_to(pull, (members, 128))], axis=1)
-    right = mm3(root, right)
-    right = 1.5 * right - 0.5 * mm3(product, right)
-    moved = right[:, :unknowns]
-    shift = jnp.sum(moved * right[:, unknowns : unknowns + 1], axis=0, keepdims=True) * inv_scale
+    right = mm3(root, spread)
+    rest = jnp.where(rows == columns, F32(0.25), 0.0) - 0.5 * product
+    moved = 1.25 * right + mm(rest.astype(BF16), right.astype(BF16))
+    pull = to_column(jnp.sum(root * pull, axis=0, keepdims=True))
+    pull = 1.5 * pull - 0.5 * to_column(jnp.sum(product * pull, axis=0, keepdims=True))
+    shift = jnp.sum(moved * pull, axis=0, keepdims=True) * inv_scale
     gain = math.sqrt(members - 1) * jnp.sqrt(inv_scale)
     result = (gain * moved + (center + shift)).astype(BF16)
     if len(block_refs) == 1:
         out_ref[...] = result
     else:
         own = members // len(block_refs)
-        for s in range(len(block_refs)):
-            out_ref[me_ref[0] ^ s] = result[s * own : (s + 1) * own]
+        out_ref[me_ref[0]] = result[:own]
+        for k, partners in enumerate(rounds_of(len(block_refs)), start=1):
+            out_ref[partner_of(partners, me_ref[0])] = result[k * own : (k + 1) * own]
 
 
 def analyse(me, lines, departure, precision, blocks, unknowns):
@@ -137,9 +170,8 @@
         pltpu.with_memory_space_constraint(mapped_prior, pltpu.HBM),
     )
     arrived = [blocks[0]]
-    for s in range(1, devices):
-        pairs = [(a, a ^ s) for a in range(devices)]
-        arrived.append(lax.ppermute(blocks[s], "mem", pairs))
+    for k, partners in enumerate(rounds_of(devices), start=1):
+        arrived.append(lax.ppermute(blocks[k], "mem", list(enumerate(partners))))
     result = analyse(me, measured_lines, departure, precision_factor, arrived, unknowns)
     result = lax.all_to_all(result, "mem", split_axis=0, concat_axis=0, tiled=True)
     return jnp.transpose(result, (1, 0, 2))

time: 38.9 us -> 36.9 us (0.949)
  blocking collectives: 12.7 us -> 10.4 us
  waiting for transfers between devices: 7.66 us -> 8.43 us
  Pallas kernels: 4.4 us -> 3.88 us
    all_to_all x1, blocking collectives: 12.7 us -> 10.4 us  [local_pairs(): lax.all_to_all(result, 'mem', split_axis=0, concat_axis=0, tiled=True)]
    ppermute x7, waiting for transfers between devices: 7.66 us -> 8.43 us  [local_pairs(): arrived.append(lax.ppermute(blocks[k], 'mem', list(enumerate(partners))))]
    pallas_call x1, Pallas kernels: 2.78 us -> 2.27 us  [analyse(): pl.pallas_call(functools.partial(analysis_kernel, unknowns), out_shape=ja...]
  transfers between devices with their start and end apart: 7 -> 7, of which waited for: 1 -> 3; matrix products, arithmetic and copies ran while one was open for 0% -> 0% of each run, Pallas kernels for 0% -> 0%
where the time goes in v3:
time: 36.9 us; the launch traced here: 36.7 us
  starting transfers between devices  12.5 us (34%)
  blocking collectives  10.4 us (28%)
  waiting for transfers between devices  8.43 us (23%)
  Pallas kernels  3.88 us (11%)
  local copies, waits for them, and re-layouts  0.74 us (2%)
  between operations  0.69 us (2%)
    ppermute x7, starting transfers between devices, local_pairs(): arrived.append(lax.ppermute(blocks[k], 'mem', list(enumerate(partners))))  12.5 us
    all_to_all x1, blocking collectives, local_pairs(): lax.all_to_all(result, 'mem', split_axis=0, concat_axis=0, tiled=True)  10.4 us
    ppermute x7, waiting for transfers between devices, local_pairs(): arrived.append(lax.ppermute(blocks[k], 'mem', list(enumerate(partners))))  8.43 us
    pallas_call x1, Pallas kernels, analyse(): pl.pallas_call(functools.partial(analysis_kernel, unknowns), out_shape=ja...  2.27 us
    pallas_call x1, Pallas kernels, local_pairs(): pl.pallas_call(pack_kernel, out_shape=[jax.ShapeDtypeStruct((own, width),...  1.61 us
  transfers between devices with their start and end apart: 7, of which 3 were waited for; matrix products, arithmetic and copies ran while one was open for 0% of the time, Pallas kernels for 0%

profile of v3, /device:TPU:0, one launch (start us, length us, event | category | flops | bytes accessed | tf_op | source)
XLA Modules:
  0.0 36.7 jit_solution(6190751360348010749)
XLA Ops:
  0.0 1.6 %shard_map.55 = (bf16[32,1280]{1,0:T(8,128)(2,1)S(1)}, bf16[32,1280]{1,0:T(8,128)(2,1)S(1)}, bf16[32,1280]{1,0:T(8,128)(2,1)S(1)}, bf16[32,1280]{1,0:T(8,128)(2,...) custom-call(s32[1]{0:T(128)} %bitcast.me_ref, ...), custom_call_target="tpu_custom_call" | custom-call | tf_op jit(solution)/shard_map/pallas_call | solution.py:156
  1.6 5.1 %collective-permute-start = (bf16[32,1280]{1,0:T(8,128)(2,1)S(1)}, bf16[32,1280]{1,0:T(8,128)(2,1)S(1)}, u32[]{:S(2)}, u32[]{:S(2)}) collective-permute-start(bf16[32,1280]{1,0:T(8,128)(2,1)S(1)} %get-tuple-element.14), channel_id=1, source_target_pairs={{0,24},{4,28},{8,16},{12,20},{16,8},{20,12},{24,0},{28,4},{1,25},{... | collective-permute-start | bytes 245768 | tf_op jit(solution)/shard_map/ppermute | solution.py:174
  6.8 0.4 collective-permute-start.1
  7.1 1.3 %collective-permute-start.2 = (bf16[32,1280]{1,0:T(8,128)(2,1)S(1)}, bf16[32,1280]{1,0:T(8,128)(2,1)S(1)}, u32[]{:S(2)}, u32[]{:S(2)}) collective-permute-start(bf16[32,1280]{1,0:T(8,128)(2,1)S(1)} %get-tuple-element.16), channel_id=1, source_target_pairs={{0,12},{4,24},{8,28},{12,0},{16,20},{20,16},{24,4},{28,8},{1,13},{... | collective-permute-start | bytes 245768 | tf_op jit(solution)/shard_map/ppermute | solution.py:174
  8.5 2.2 %collective-permute-start.3 = (bf16[32,1280]{1,0:T(8,128)(2,1)S(1)}, bf16[32,1280]{1,0:T(8,128)(2,1)S(1)}, u32[]{:S(2)}, u32[]{:S(2)}) collective-permute-start(bf16[32,1280]{1,0:T(8,128)(2,1)S(1)} %get-tuple-element.17), channel_id=1, source_target_pairs={{0,28},{4,12},{8,20},{12,4},{16,24},{20,8},{24,16},{28,0},{1,29},{... | collective-permute-start | bytes 245768 | tf_op jit(solution)/shard_map/ppermute | solution.py:174
  10.7 0.0 copy-start.1
  10.7 0.0 copy-start
  10.7 1.4 %collective-permute-start.4 = (bf16[32,1280]{1,0:T(8,128)(2,1)S(1)}, bf16[32,1280]{1,0:T(8,128)(2,1)S(1)}, u32[]{:S(2)}, u32[]{:S(2)}) collective-permute-start(bf16[32,1280]{1,0:T(8,128)(2,1)S(1)} %get-tuple-element.18), channel_id=1, source_target_pairs={{0,16},{4,8},{8,4},{12,24},{16,0},{20,28},{24,12},{28,20},{1,17},{... | collective-permute-start | bytes 245768 | tf_op jit(solution)/shard_map/ppermute | solution.py:174
  12.1 0.0 collective-permute-done.refs_1_
  12.1 2.0 %collective-permute-start.5 = (bf16[32,1280]{1,0:T(8,128)(2,1)S(1)}, bf16[32,1280]{1,0:T(8,128)(2,1)S(1)}, u32[]{:S(2)}, u32[]{:S(2)}) collective-permute-start(bf16[32,1280]{1,0:T(8,128)(2,1)S(1)} %get-tuple-element.19), channel_id=1, source_target_pairs={{0,4},{4,0},{8,12},{12,8},{16,28},{20,24},{24,20},{28,16},{1,5},{5... | collective-permute-start | bytes 245768 | tf_op jit(solution)/shard_map/ppermute | solution.py:174
  14.1 4.7 %collective-permute-done.1.refs_2_ = bf16[32,1280]{1,0:T(8,128)(2,1)S(1)} collective-permute-done((bf16[32,1280]{1,0:T(8,128)(2,1)S(1)}, bf16[32,1280]{1,0:T(8,128)(2,1)S(1)}, u32[]{:S(2)}, u32[]{:S(2)}) %collective-permute-start.1) | collective-permute-done | bytes 81952 | tf_op jit(solution)/shard_map/ppermute | solution.py:174
  18.8 0.0 collective-permute-start.6
  19.4 0.0 collective-permute-done.2.refs_3_
  19.4 0.0 collective-permute-done.3.refs_4_
  19.5 0.2 collective-permute-done.4.refs_5_
  19.7 0.0 collective-permute-done.5.refs_6_
  19.7 3.6 %collective-permute-done.6.refs_7_ = bf16[32,1280]{1,0:T(8,128)(2,1)S(1)} collective-permute-done((bf16[32,1280]{1,0:T(8,128)(2,1)S(1)}, bf16[32,1280]{1,0:T(8,128)(2,1)S(1)}, u32[]{:S(2)}, u32[]{:S(2)}) %collective-permute-start.6) | collective-permute-done | bytes 81952 | tf_op jit(solution)/shard_map/ppermute | solution.py:174
  23.2 0.0 copy-done.1
  23.2 0.0 copy-done
  23.2 2.3 %shard_map.56 = bf16[8,32,256]{2,1,0:T(8,128)(2,1)S(1)} custom-call(s32[1]{0:T(128)} %bitcast.me_ref, s32[1]{0:T(128)S(6)} %copy.7.lines_ref, f32[1,1024]{1,0:T(1,128)S(1)} %copy-done, f32[1,1024]{1,0:T(1,128)S(1)} %copy-done.1, bf16[32,1280]{1,0:T(8,128)(2,1)S(1)} %get-tuple-element.13.refs_0_, bf16[32,1280]{1,0:T(8,128)(2,1)S(1)} %collective-permute-done.refs_1_, ...), custom_call_target="tpu_custom_call" | custom-call | tf_op jit(solution)/shard_map/pallas_call | solution.py:143
  25.5 10.4 %all_to_all.5 = bf16[8,32,256]{2,1,0:T(8,128)(2,1)S(1)} all-to-all(bf16[8,32,256]{2,1,0:T(8,128)(2,1)S(1)} %shard_map.56), channel_id=1, replica_groups=mesh['mem'=8,'grp'=4] {'mem'}, dimensions={0} | all-to-all | bytes 262144 | tf_op jit(solution)/shard_map/all_to_all | solution.py:176
  35.9 0.7 %copy.6 = bf16[32,8,256]{2,1,0:T(8,128)(2,1)} copy(bf16[32,8,256]{2,0,1:T(8,128)(2,1)S(1)} %bitcast.2) | data formatting | bytes 262144 | tf_op jit(solution)/shard_map/transpose | solution.py:177
Async XLA Ops:
  1.6 10.5 %collective-permute-start = (bf16[32,1280]{1,0:T(8,128)(2,1)S(1)}, bf16[32,1280]{1,0:T(8,128)(2,1)S(1)}, u32[]{:S(2)}, u32[]{:S(2)}) collective-permute-start(bf16[32,1280]{1,0:T(8,128)(2,1)S(1)} %get-tuple-element.14), channel_id=1, source_target_pairs={{0,24},{4,28},{8,16},{12,20},{16,8},{20,12},{24,0},{28,4},{1,25},{... | collective-permute-start | bytes 245768 | tf_op jit(solution)/shard_map/ppermute | solution.py:174
  6.8 12.0 %collective-permute-start.1 = (bf16[32,1280]{1,0:T(8,128)(2,1)S(1)}, bf16[32,1280]{1,0:T(8,128)(2,1)S(1)}, u32[]{:S(2)}, u32[]{:S(2)}) collective-permute-start(bf16[32,1280]{1,0:T(8,128)(2,1)S(1)} %get-tuple-element.15), channel_id=1, source_target_pairs={{0,20},{4,16},{8,24},{12,28},{16,4},{20,0},{24,8},{28,12},{1,21},{... | collective-permute-start | bytes 245768 | tf_op jit(solution)/shard_map/ppermute | solution.py:174
  7.1 12.3 %collective-permute-start.2 = (bf16[32,1280]{1,0:T(8,128)(2,1)S(1)}, bf16[32,1280]{1,0:T(8,128)(2,1)S(1)}, u32[]{:S(2)}, u32[]{:S(2)}) collective-permute-start(bf16[32,1280]{1,0:T(8,128)(2,1)S(1)} %get-tuple-element.16), channel_id=1, source_target_pairs={{0,12},{4,24},{8,28},{12,0},{16,20},{20,16},{24,4},{28,8},{1,13},{... | collective-permute-start | bytes 245768 | tf_op jit(solution)/shard_map/ppermute | solution.py:174
  8.5 11.0 %collective-permute-start.3 = (bf16[32,1280]{1,0:T(8,128)(2,1)S(1)}, bf16[32,1280]{1,0:T(8,128)(2,1)S(1)}, u32[]{:S(2)}, u32[]{:S(2)}) collective-permute-start(bf16[32,1280]{1,0:T(8,128)(2,1)S(1)} %get-tuple-element.17), channel_id=1, source_target_pairs={{0,28},{4,12},{8,20},{12,4},{16,24},{20,8},{24,16},{28,0},{1,29},{... | collective-permute-start | bytes 245768 | tf_op jit(solution)/shard_map/ppermute | solution.py:174
  10.7 12.6 %copy-start.1 = (f32[1,1024]{1,0:T(1,128)S(1)}, f32[1,1024]{1,0:T(1,128)}, u32[]{:S(2)}) copy-start(f32[1,1024]{1,0:T(1,128)} %precision_ref.1) | copy-start | bytes 12292
  10.7 12.6 %copy-start = (f32[1,1024]{1,0:T(1,128)S(1)}, f32[1,1024]{1,0:T(1,128)}, u32[]{:S(2)}) copy-start(f32[1,1024]{1,0:T(1,128)} %departure_ref.1) | copy-start | bytes 12292
  10.7 9.0 %collective-permute-start.4 = (bf16[32,1280]{1,0:T(8,128)(2,1)S(1)}, bf16[32,1280]{1,0:T(8,128)(2,1)S(1)}, u32[]{:S(2)}, u32[]{:S(2)}) collective-permute-start(bf16[32,1280]{1,0:T(8,128)(2,1)S(1)} %get-tuple-element.18), channel_id=1, source_target_pairs={{0,16},{4,8},{8,4},{12,24},{16,0},{20,28},{24,12},{28,20},{1,17},{... | collective-permute-start | bytes 245768 | tf_op jit(solution)/shard_map/ppermute | solution.py:174
  12.1 7.6 %collective-permute-start.5 = (bf16[32,1280]{1,0:T(8,128)(2,1)S(1)}, bf16[32,1280]{1,0:T(8,128)(2,1)S(1)}, u32[]{:S(2)}, u32[]{:S(2)}) collective-permute-start(bf16[32,1280]{1,0:T(8,128)(2,1)S(1)} %get-tuple-element.19), channel_id=1, source_target_pairs={{0,4},{4,0},{8,12},{12,8},{16,28},{20,24},{24,20},{28,16},{1,5},{5... | collective-permute-start | bytes 245768 | tf_op jit(solution)/shard_map/ppermute | solution.py:174
  18.8 4.4 %collective-permute-start.6 = (bf16[32,1280]{1,0:T(8,128)(2,1)S(1)}, bf16[32,1280]{1,0:T(8,128)(2,1)S(1)}, u32[]{:S(2)}, u32[]{:S(2)}) collective-permute-start(bf16[32,1280]{1,0:T(8,128)(2,1)S(1)} %get-tuple-element.20), channel_id=1, source_target_pairs={{0,8},{4,20},{8,0},{12,16},{16,12},{20,4},{24,28},{28,24},{1,9},{5... | collective-permute-start | bytes 245768 | tf_op jit(solution)/shard_map/ppermute | solution.py:174

commit v4 on v3

--- a/solution.py
+++ b/solution.py
@@ -37,6 +37,16 @@
 def split(x):
     high = x.astype(BF16)
     return high, (x - high.astype(F32)).astype(BF16)
+
+
+def left(a, b):
+    high, low = split(b)
+    return mm(a, high) + mm(a, low)
+
+
+def right(a, b):
+    high, low = split(a)
+    return mm(high, b) + mm(low, b)
 
 
 def mm3(a, b):
@@ -94,36 +104,35 @@
     weights = jnp.where(row_ids < lines_ref[0], precision_ref[...], 0.0)
     root_weights = jnp.sqrt(weights)
     scaled = deviat * root_weights
-    half = scaled.astype(BF16)
-    gram = mm(half, half, (1, 1))
-    pull = jnp.sum(scaled * (root_weights * departure_ref[...]), axis=1, keepdims=True)
+    scaled = scaled.astype(BF16)
+    gram = mm(scaled, scaled, (1, 1))
+    pull = scaled.astype(F32) * (root_weights * departure_ref[...])
+    pull = jnp.sum(pull, axis=1, keepdims=True)
 
     rows = lax.broadcasted_iota(jnp.int32, (members, members), 0)
     columns = lax.broadcasted_iota(jnp.int32, (members, members), 1)
 
-    def to_column(row):
+    def times(matrix, column):
+        row = jnp.sum(matrix * column, axis=0, keepdims=True)
         return jnp.sum(jnp.where(rows == columns, row, 0.0), axis=1, keepdims=True)
 
     system = gram + jnp.where(rows == columns, F32(members - 1), 0.0)
     norm2 = jnp.sum(jnp.sum(system * system, axis=0, keepdims=True), axis=1, keepdims=True)
     inv_scale = lax.rsqrt(norm2)
     iterate = system * inv_scale
-    low = system.astype(BF16)
-    square = mm(low, low) * (inv_scale * inv_scale)
-    root = jnp.where(rows == columns, F32(1.5), 0.0) - 0.5 * iterate
-    iterate = 1.5 * iterate - 0.5 * square
+    product = iterate.astype(BF16)
+    root = jnp.where(rows == columns, F32(1.5), 0.0) - 0.5 * product.astype(F32)
+    iterate = 1.5 * iterate - 0.5 * right(iterate, product)
     for _ in range(1, ITERS - 1):
-        root_low, iterate_low = root.astype(BF16), iterate.astype(BF16)
-        product = mm(root_low, iterate_low).astype(BF16)
-        iterate = 1.5 * iterate - 0.5 * mm(iterate_low, product)
-        root = 1.5 * root - 0.5 * mm(product, root_low)
-    product = mm(root.astype(BF16), iterate.astype(BF16))
-    right = mm3(root, spread)
-    rest = jnp.where(rows == columns, F32(0.25), 0.0) - 0.5 * product
-    moved = 1.25 * right + mm(rest.astype(BF16), right.astype(BF16))
-    pull = to_column(jnp.sum(root * pull, axis=0, keepdims=True))
-    pull = 1.5 * pull - 0.5 * to_column(jnp.sum(product * pull, axis=0, keepdims=True))
-    shift = jnp.sum(moved * pull, axis=0, keepdims=True) * inv_scale
+        product = mm(root.astype(BF16), iterate.astype(BF16)).astype(BF16)
+        iterate = 1.5 * iterate - 0.5 * right(iterate, product)
+        root = 1.5 * root - 0.5 * left(product, root)
+    product = mm3(root, iterate)
+    moved = right(root, spread.astype(BF16))
+    moved = 1.5 * moved - 0.5 * mm3(product, moved)
+    pull = times(root, pull)
+    pull = 1.5 * pull - 0.5 * times(product, pull)
+    shift = jnp.sum(moved * (pull * inv_scale), axis=0, keepdims=True)
     gain = math.sqrt(members - 1) * jnp.sqrt(inv_scale)
     result = (gain * moved + (center + shift)).astype(BF16)
     if len(block_refs) == 1:

time: 36.9 us -> 37.4 us (1.014)
  Pallas kernels: 3.88 us -> 4.41 us
    pallas_call x1, Pallas kernels: 2.27 us -> 2.79 us  [analyse(): pl.pallas_call(functools.partial(analysis_kernel, unknowns), out_shape=ja...]
where the time goes in v4:
time: 37.4 us; the launch traced here: 37.2 us
  starting transfers between devices  12.5 us (33%)
  blocking collectives  10.4 us (28%)
  waiting for transfers between devices  8.43 us (23%)
  Pallas kernels  4.41 us (12%)
  local copies, waits for them, and re-layouts  0.74 us (2%)
  between operations  0.69 us (2%)
    ppermute x7, starting transfers between devices, local_pairs(): arrived.append(lax.ppermute(blocks[k], 'mem', list(enumerate(partners))))  12.5 us
    all_to_all x1, blocking collectives, local_pairs(): lax.all_to_all(result, 'mem', split_axis=0, concat_axis=0, tiled=True)  10.4 us
    ppermute x7, waiting for transfers between devices, local_pairs(): arrived.append(lax.ppermute(blocks[k], 'mem', list(enumerate(partners))))  8.43 us
    pallas_call x1, Pallas kernels, analyse(): pl.pallas_call(functools.partial(analysis_kernel, unknowns), out_shape=ja...  2.79 us
    pallas_call x1, Pallas kernels, local_pairs(): pl.pallas_call(pack_kernel, out_shape=[jax.ShapeDtypeStruct((own, width),...  1.61 us
  transfers between devices with their start and end apart: 7, of which 3 were waited for; matrix products, arithmetic and copies ran while one was open for 0% of the time, Pallas kernels for 0%

profile of v4, /device:TPU:0, one launch (start us, length us, event | category | flops | bytes accessed | tf_op | source)
XLA Modules:
  0.0 37.2 jit_solution(4760631127298613023)
XLA Ops:
  0.0 1.6 %shard_map.55 = (bf16[32,1280]{1,0:T(8,128)(2,1)S(1)}, bf16[32,1280]{1,0:T(8,128)(2,1)S(1)}, bf16[32,1280]{1,0:T(8,128)(2,1)S(1)}, bf16[32,1280]{1,0:T(8,128)(2,...) custom-call(s32[1]{0:T(128)} %bitcast.me_ref, ...), custom_call_target="tpu_custom_call" | custom-call | tf_op jit(solution)/shard_map/pallas_call | solution.py:165
  1.6 5.1 %collective-permute-start = (bf16[32,1280]{1,0:T(8,128)(2,1)S(1)}, bf16[32,1280]{1,0:T(8,128)(2,1)S(1)}, u32[]{:S(2)}, u32[]{:S(2)}) collective-permute-start(bf16[32,1280]{1,0:T(8,128)(2,1)S(1)} %get-tuple-element.14), channel_id=1, source_target_pairs={{0,24},{4,28},{8,16},{12,20},{16,8},{20,12},{24,0},{28,4},{1,25},{... | collective-permute-start | bytes 245768 | tf_op jit(solution)/shard_map/ppermute | solution.py:183
  6.8 0.4 collective-permute-start.1
  7.1 1.3 %collective-permute-start.2 = (bf16[32,1280]{1,0:T(8,128)(2,1)S(1)}, bf16[32,1280]{1,0:T(8,128)(2,1)S(1)}, u32[]{:S(2)}, u32[]{:S(2)}) collective-permute-start(bf16[32,1280]{1,0:T(8,128)(2,1)S(1)} %get-tuple-element.16), channel_id=1, source_target_pairs={{0,12},{4,24},{8,28},{12,0},{16,20},{20,16},{24,4},{28,8},{1,13},{... | collective-permute-start | bytes 245768 | tf_op jit(solution)/shard_map/ppermute | solution.py:183
  8.5 2.2 %collective-permute-start.3 = (bf16[32,1280]{1,0:T(8,128)(2,1)S(1)}, bf16[32,1280]{1,0:T(8,128)(2,1)S(1)}, u32[]{:S(2)}, u32[]{:S(2)}) collective-permute-start(bf16[32,1280]{1,0:T(8,128)(2,1)S(1)} %get-tuple-element.17), channel_id=1, source_target_pairs={{0,28},{4,12},{8,20},{12,4},{16,24},{20,8},{24,16},{28,0},{1,29},{... | collective-permute-start | bytes 245768 | tf_op jit(solution)/shard_map/ppermute | solution.py:183
  10.7 0.0 copy-start.1
  10.7 0.0 copy-start
  10.7 1.4 %collective-permute-start.4 = (bf16[32,1280]{1,0:T(8,128)(2,1)S(1)}, bf16[32,1280]{1,0:T(8,128)(2,1)S(1)}, u32[]{:S(2)}, u32[]{:S(2)}) collective-permute-start(bf16[32,1280]{1,0:T(8,128)(2,1)S(1)} %get-tuple-element.18), channel_id=1, source_target_pairs={{0,16},{4,8},{8,4},{12,24},{16,0},{20,28},{24,12},{28,20},{1,17},{... | collective-permute-start | bytes 245768 | tf_op jit(solution)/shard_map/ppermute | solution.py:183
  12.1 0.0 collective-permute-done.refs_1_
  12.1 2.0 %collective-permute-start.5 = (bf16[32,1280]{1,0:T(8,128)(2,1)S(1)}, bf16[32,1280]{1,0:T(8,128)(2,1)S(1)}, u32[]{:S(2)}, u32[]{:S(2)}) collective-permute-start(bf16[32,1280]{1,0:T(8,128)(2,1)S(1)} %get-tuple-element.19), channel_id=1, source_target_pairs={{0,4},{4,0},{8,12},{12,8},{16,28},{20,24},{24,20},{28,16},{1,5},{5... | collective-permute-start | bytes 245768 | tf_op jit(solution)/shard_map/ppermute | solution.py:183
  14.1 4.7 %collective-permute-done.1.refs_2_ = bf16[32,1280]{1,0:T(8,128)(2,1)S(1)} collective-permute-done((bf16[32,1280]{1,0:T(8,128)(2,1)S(1)}, bf16[32,1280]{1,0:T(8,128)(2,1)S(1)}, u32[]{:S(2)}, u32[]{:S(2)}) %collective-permute-start.1) | collective-permute-done | bytes 81952 | tf_op jit(solution)/shard_map/ppermute | solution.py:183
  18.8 0.0 collective-permute-start.6
  19.4 0.0 collective-permute-done.2.refs_3_
  19.4 0.0 collective-permute-done.3.refs_4_
  19.5 0.2 collective-permute-done.4.refs_5_
  19.7 0.0 collective-permute-done.5.refs_6_
  19.7 3.6 %collective-permute-done.6.refs_7_ = bf16[32,1280]{1,0:T(8,128)(2,1)S(1)} collective-permute-done((bf16[32,1280]{1,0:T(8,128)(2,1)S(1)}, bf16[32,1280]{1,0:T(8,128)(2,1)S(1)}, u32[]{:S(2)}, u32[]{:S(2)}) %collective-permute-start.6) | collective-permute-done | bytes 81952 | tf_op jit(solution)/shard_map/ppermute | solution.py:183
  23.2 0.0 copy-done.1
  23.2 0.0 copy-done
  23.2 2.8 %shard_map.56 = bf16[8,32,256]{2,1,0:T(8,128)(2,1)S(1)} custom-call(s32[1]{0:T(128)} %bitcast.me_ref, s32[1]{0:T(128)S(6)} %copy.7.lines_ref, f32[1,1024]{1,0:T(1,128)S(1)} %copy-done, f32[1,1024]{1,0:T(1,128)S(1)} %copy-done.1, bf16[32,1280]{1,0:T(8,128)(2,1)S(1)} %get-tuple-element.13.refs_0_, bf16[32,1280]{1,0:T(8,128)(2,1)S(1)} %collective-permute-done.refs_1_, ...), custom_call_target="tpu_custom_call" | custom-call | tf_op jit(solution)/shard_map/pallas_call | solution.py:152
  26.0 10.4 %all_to_all.5 = bf16[8,32,256]{2,1,0:T(8,128)(2,1)S(1)} all-to-all(bf16[8,32,256]{2,1,0:T(8,128)(2,1)S(1)} %shard_map.56), channel_id=1, replica_groups=mesh['mem'=8,'grp'=4] {'mem'}, dimensions={0} | all-to-all | bytes 262144 | tf_op jit(solution)/shard_map/all_to_all | solution.py:185
  36.5 0.7 %copy.6 = bf16[32,8,256]{2,1,0:T(8,128)(2,1)} copy(bf16[32,8,256]{2,0,1:T(8,128)(2,1)S(1)} %bitcast.2) | data formatting | bytes 262144 | tf_op jit(solution)/shard_map/transpose | solution.py:186
Async XLA Ops:
  1.6 10.5 %collective-permute-start = (bf16[32,1280]{1,0:T(8,128)(2,1)S(1)}, bf16[32,1280]{1,0:T(8,128)(2,1)S(1)}, u32[]{:S(2)}, u32[]{:S(2)}) collective-permute-start(bf16[32,1280]{1,0:T(8,128)(2,1)S(1)} %get-tuple-element.14), channel_id=1, source_target_pairs={{0,24},{4,28},{8,16},{12,20},{16,8},{20,12},{24,0},{28,4},{1,25},{... | collective-permute-start | bytes 245768 | tf_op jit(solution)/shard_map/ppermute | solution.py:183
  6.8 12.0 %collective-permute-start.1 = (bf16[32,1280]{1,0:T(8,128)(2,1)S(1)}, bf16[32,1280]{1,0:T(8,128)(2,1)S(1)}, u32[]{:S(2)}, u32[]{:S(2)}) collective-permute-start(bf16[32,1280]{1,0:T(8,128)(2,1)S(1)} %get-tuple-element.15), channel_id=1, source_target_pairs={{0,20},{4,16},{8,24},{12,28},{16,4},{20,0},{24,8},{28,12},{1,21},{... | collective-permute-start | bytes 245768 | tf_op jit(solution)/shard_map/ppermute | solution.py:183
  7.1 12.3 %collective-permute-start.2 = (bf16[32,1280]{1,0:T(8,128)(2,1)S(1)}, bf16[32,1280]{1,0:T(8,128)(2,1)S(1)}, u32[]{:S(2)}, u32[]{:S(2)}) collective-permute-start(bf16[32,1280]{1,0:T(8,128)(2,1)S(1)} %get-tuple-element.16), channel_id=1, source_target_pairs={{0,12},{4,24},{8,28},{12,0},{16,20},{20,16},{24,4},{28,8},{1,13},{... | collective-permute-start | bytes 245768 | tf_op jit(solution)/shard_map/ppermute | solution.py:183
  8.5 11.0 %collective-permute-start.3 = (bf16[32,1280]{1,0:T(8,128)(2,1)S(1)}, bf16[32,1280]{1,0:T(8,128)(2,1)S(1)}, u32[]{:S(2)}, u32[]{:S(2)}) collective-permute-start(bf16[32,1280]{1,0:T(8,128)(2,1)S(1)} %get-tuple-element.17), channel_id=1, source_target_pairs={{0,28},{4,12},{8,20},{12,4},{16,24},{20,8},{24,16},{28,0},{1,29},{... | collective-permute-start | bytes 245768 | tf_op jit(solution)/shard_map/ppermute | solution.py:183
  10.7 12.6 %copy-start.1 = (f32[1,1024]{1,0:T(1,128)S(1)}, f32[1,1024]{1,0:T(1,128)}, u32[]{:S(2)}) copy-start(f32[1,1024]{1,0:T(1,128)} %precision_ref.1) | copy-start | bytes 12292
  10.7 12.6 %copy-start = (f32[1,1024]{1,0:T(1,128)S(1)}, f32[1,1024]{1,0:T(1,128)}, u32[]{:S(2)}) copy-start(f32[1,1024]{1,0:T(1,128)} %departure_ref.1) | copy-start | bytes 12292
  10.7 9.0 %collective-permute-start.4 = (bf16[32,1280]{1,0:T(8,128)(2,1)S(1)}, bf16[32,1280]{1,0:T(8,128)(2,1)S(1)}, u32[]{:S(2)}, u32[]{:S(2)}) collective-permute-start(bf16[32,1280]{1,0:T(8,128)(2,1)S(1)} %get-tuple-element.18), channel_id=1, source_target_pairs={{0,16},{4,8},{8,4},{12,24},{16,0},{20,28},{24,12},{28,20},{1,17},{... | collective-permute-start | bytes 245768 | tf_op jit(solution)/shard_map/ppermute | solution.py:183
  12.1 7.6 %collective-permute-start.5 = (bf16[32,1280]{1,0:T(8,128)(2,1)S(1)}, bf16[32,1280]{1,0:T(8,128)(2,1)S(1)}, u32[]{:S(2)}, u32[]{:S(2)}) collective-permute-start(bf16[32,1280]{1,0:T(8,128)(2,1)S(1)} %get-tuple-element.19), channel_id=1, source_target_pairs={{0,4},{4,0},{8,12},{12,8},{16,28},{20,24},{24,20},{28,16},{1,5},{5... | collective-permute-start | bytes 245768 | tf_op jit(solution)/shard_map/ppermute | solution.py:183
  18.8 4.4 %collective-permute-start.6 = (bf16[32,1280]{1,0:T(8,128)(2,1)S(1)}, bf16[32,1280]{1,0:T(8,128)(2,1)S(1)}, u32[]{:S(2)}, u32[]{:S(2)}) collective-permute-start(bf16[32,1280]{1,0:T(8,128)(2,1)S(1)} %get-tuple-element.20), channel_id=1, source_target_pairs={{0,8},{4,20},{8,0},{12,16},{16,12},{20,4},{24,28},{28,24},{1,9},{5... | collective-permute-start | bytes 245768 | tf_op jit(solution)/shard_map/ppermute | solution.py:183

commit v5 on v4

--- a/solution.py
+++ b/solution.py
@@ -119,10 +119,10 @@
     system = gram + jnp.where(rows == columns, F32(members - 1), 0.0)
     norm2 = jnp.sum(jnp.sum(system * system, axis=0, keepdims=True), axis=1, keepdims=True)
     inv_scale = lax.rsqrt(norm2)
-    iterate = system * inv_scale
-    product = iterate.astype(BF16)
-    root = jnp.where(rows == columns, F32(1.5), 0.0) - 0.5 * product.astype(F32)
-    iterate = 1.5 * iterate - 0.5 * right(iterate, product)
+    product = system.astype(BF16)
+    square = right(system, product)
+    root = jnp.where(rows == columns, F32(1.5), 0.0) - 0.5 * inv_scale * product.astype(F32)
+    iterate = inv_scale * (1.5 * system - 0.5 * inv_scale * square)
     for _ in range(1, ITERS - 1):
         product = mm(root.astype(BF16), iterate.astype(BF16)).astype(BF16)
         iterate = 1.5 * iterate - 0.5 * right(iterate, product)

time: 37.4 us -> 37.3 us (level)
  no operation moved by 1% of the time
where the time goes in v5:
time: 37.3 us; the launch traced here: 37.1 us
  starting transfers between devices  12.5 us (34%)
  blocking collectives  10.4 us (28%)
  waiting for transfers between devices  8.43 us (23%)
  Pallas kernels  4.29 us (12%)
  local copies, waits for them, and re-layouts  0.74 us (2%)
  between operations  0.69 us (2%)
    ppermute x7, starting transfers between devices, local_pairs(): arrived.append(lax.ppermute(blocks[k], 'mem', list(enumerate(partners))))  12.5 us
    all_to_all x1, blocking collectives, local_pairs(): lax.all_to_all(result, 'mem', split_axis=0, concat_axis=0, tiled=True)  10.4 us
    ppermute x7, waiting for transfers between devices, local_pairs(): arrived.append(lax.ppermute(blocks[k], 'mem', list(enumerate(partners))))  8.43 us
    pallas_call x1, Pallas kernels, analyse(): pl.pallas_call(functools.partial(analysis_kernel, unknowns), out_shape=ja...  2.67 us
    pallas_call x1, Pallas kernels, local_pairs(): pl.pallas_call(pack_kernel, out_shape=[jax.ShapeDtypeStruct((own, width),...  1.61 us
  transfers between devices with their start and end apart: 7, of which 3 were waited for; matrix products, arithmetic and copies ran while one was open for 0% of the time, Pallas kernels for 0%

profile of v5, /device:TPU:0, one launch (start us, length us, event | category | flops | bytes accessed | tf_op | source)
XLA Modules:
  0.0 37.1 jit_solution(7175030978451380994)
XLA Ops:
  0.0 1.6 %shard_map.55 = (bf16[32,1280]{1,0:T(8,128)(2,1)S(1)}, bf16[32,1280]{1,0:T(8,128)(2,1)S(1)}, bf16[32,1280]{1,0:T(8,128)(2,1)S(1)}, bf16[32,1280]{1,0:T(8,128)(2,...) custom-call(s32[1]{0:T(128)} %bitcast.me_ref, ...), custom_call_target="tpu_custom_call" | custom-call | tf_op jit(solution)/shard_map/pallas_call | solution.py:165
  1.6 5.1 %collective-permute-start = (bf16[32,1280]{1,0:T(8,128)(2,1)S(1)}, bf16[32,1280]{1,0:T(8,128)(2,1)S(1)}, u32[]{:S(2)}, u32[]{:S(2)}) collective-permute-start(bf16[32,1280]{1,0:T(8,128)(2,1)S(1)} %get-tuple-element.14), channel_id=1, source_target_pairs={{0,24},{4,28},{8,16},{12,20},{16,8},{20,12},{24,0},{28,4},{1,25},{... | collective-permute-start | bytes 245768 | tf_op jit(solution)/shard_map/ppermute | solution.py:183
  6.8 0.4 collective-permute-start.1
  7.1 1.3 %collective-permute-start.2 = (bf16[32,1280]{1,0:T(8,128)(2,1)S(1)}, bf16[32,1280]{1,0:T(8,128)(2,1)S(1)}, u32[]{:S(2)}, u32[]{:S(2)}) collective-permute-start(bf16[32,1280]{1,0:T(8,128)(2,1)S(1)} %get-tuple-element.16), channel_id=1, source_target_pairs={{0,12},{4,24},{8,28},{12,0},{16,20},{20,16},{24,4},{28,8},{1,13},{... | collective-permute-start | bytes 245768 | tf_op jit(solution)/shard_map/ppermute | solution.py:183
  8.5 2.2 %collective-permute-start.3 = (bf16[32,1280]{1,0:T(8,128)(2,1)S(1)}, bf16[32,1280]{1,0:T(8,128)(2,1)S(1)}, u32[]{:S(2)}, u32[]{:S(2)}) collective-permute-start(bf16[32,1280]{1,0:T(8,128)(2,1)S(1)} %get-tuple-element.17), channel_id=1, source_target_pairs={{0,28},{4,12},{8,20},{12,4},{16,24},{20,8},{24,16},{28,0},{1,29},{... | collective-permute-start | bytes 245768 | tf_op jit(solution)/shard_map/ppermute | solution.py:183
  10.7 0.0 copy-start.1
  10.7 0.0 copy-start
  10.7 1.4 %collective-permute-start.4 = (bf16[32,1280]{1,0:T(8,128)(2,1)S(1)}, bf16[32,1280]{1,0:T(8,128)(2,1)S(1)}, u32[]{:S(2)}, u32[]{:S(2)}) collective-permute-start(bf16[32,1280]{1,0:T(8,128)(2,1)S(1)} %get-tuple-element.18), channel_id=1, source_target_pairs={{0,16},{4,8},{8,4},{12,24},{16,0},{20,28},{24,12},{28,20},{1,17},{... | collective-permute-start | bytes 245768 | tf_op jit(solution)/shard_map/ppermute | solution.py:183
  12.1 0.0 collective-permute-done.refs_1_
  12.1 2.0 %collective-permute-start.5 = (bf16[32,1280]{1,0:T(8,128)(2,1)S(1)}, bf16[32,1280]{1,0:T(8,128)(2,1)S(1)}, u32[]{:S(2)}, u32[]{:S(2)}) collective-permute-start(bf16[32,1280]{1,0:T(8,128)(2,1)S(1)} %get-tuple-element.19), channel_id=1, source_target_pairs={{0,4},{4,0},{8,12},{12,8},{16,28},{20,24},{24,20},{28,16},{1,5},{5... | collective-permute-start | bytes 245768 | tf_op jit(solution)/shard_map/ppermute | solution.py:183
  14.1 4.7 %collective-permute-done.1.refs_2_ = bf16[32,1280]{1,0:T(8,128)(2,1)S(1)} collective-permute-done((bf16[32,1280]{1,0:T(8,128)(2,1)S(1)}, bf16[32,1280]{1,0:T(8,128)(2,1)S(1)}, u32[]{:S(2)}, u32[]{:S(2)}) %collective-permute-start.1) | collective-permute-done | bytes 81952 | tf_op jit(solution)/shard_map/ppermute | solution.py:183
  18.8 0.0 collective-permute-start.6
  19.4 0.0 collective-permute-done.2.refs_3_
  19.4 0.0 collective-permute-done.3.refs_4_
  19.5 0.2 collective-permute-done.4.refs_5_
  19.7 0.0 collective-permute-done.5.refs_6_
  19.7 3.6 %collective-permute-done.6.refs_7_ = bf16[32,1280]{1,0:T(8,128)(2,1)S(1)} collective-permute-done((bf16[32,1280]{1,0:T(8,128)(2,1)S(1)}, bf16[32,1280]{1,0:T(8,128)(2,1)S(1)}, u32[]{:S(2)}, u32[]{:S(2)}) %collective-permute-start.6) | collective-permute-done | bytes 81952 | tf_op jit(solution)/shard_map/ppermute | solution.py:183
  23.2 0.0 copy-done.1
  23.2 0.0 copy-done
  23.2 2.7 %shard_map.56 = bf16[8,32,256]{2,1,0:T(8,128)(2,1)S(1)} custom-call(s32[1]{0:T(128)} %bitcast.me_ref, s32[1]{0:T(128)S(6)} %copy.7.lines_ref, f32[1,1024]{1,0:T(1,128)S(1)} %copy-done, f32[1,1024]{1,0:T(1,128)S(1)} %copy-done.1, bf16[32,1280]{1,0:T(8,128)(2,1)S(1)} %get-tuple-element.13.refs_0_, bf16[32,1280]{1,0:T(8,128)(2,1)S(1)} %collective-permute-done.refs_1_, ...), custom_call_target="tpu_custom_call" | custom-call | tf_op jit(solution)/shard_map/pallas_call | solution.py:152
  25.9 10.4 %all_to_all.5 = bf16[8,32,256]{2,1,0:T(8,128)(2,1)S(1)} all-to-all(bf16[8,32,256]{2,1,0:T(8,128)(2,1)S(1)} %shard_map.56), channel_id=1, replica_groups=mesh['mem'=8,'grp'=4] {'mem'}, dimensions={0} | all-to-all | bytes 262144 | tf_op jit(solution)/shard_map/all_to_all | solution.py:185
  36.4 0.7 %copy.6 = bf16[32,8,256]{2,1,0:T(8,128)(2,1)} copy(bf16[32,8,256]{2,0,1:T(8,128)(2,1)S(1)} %bitcast.2) | data formatting | bytes 262144 | tf_op jit(solution)/shard_map/transpose | solution.py:186
Async XLA Ops:
  1.6 10.5 %collective-permute-start = (bf16[32,1280]{1,0:T(8,128)(2,1)S(1)}, bf16[32,1280]{1,0:T(8,128)(2,1)S(1)}, u32[]{:S(2)}, u32[]{:S(2)}) collective-permute-start(bf16[32,1280]{1,0:T(8,128)(2,1)S(1)} %get-tuple-element.14), channel_id=1, source_target_pairs={{0,24},{4,28},{8,16},{12,20},{16,8},{20,12},{24,0},{28,4},{1,25},{... | collective-permute-start | bytes 245768 | tf_op jit(solution)/shard_map/ppermute | solution.py:183
  6.8 12.0 %collective-permute-start.1 = (bf16[32,1280]{1,0:T(8,128)(2,1)S(1)}, bf16[32,1280]{1,0:T(8,128)(2,1)S(1)}, u32[]{:S(2)}, u32[]{:S(2)}) collective-permute-start(bf16[32,1280]{1,0:T(8,128)(2,1)S(1)} %get-tuple-element.15), channel_id=1, source_target_pairs={{0,20},{4,16},{8,24},{12,28},{16,4},{20,0},{24,8},{28,12},{1,21},{... | collective-permute-start | bytes 245768 | tf_op jit(solution)/shard_map/ppermute | solution.py:183
  7.1 12.3 %collective-permute-start.2 = (bf16[32,1280]{1,0:T(8,128)(2,1)S(1)}, bf16[32,1280]{1,0:T(8,128)(2,1)S(1)}, u32[]{:S(2)}, u32[]{:S(2)}) collective-permute-start(bf16[32,1280]{1,0:T(8,128)(2,1)S(1)} %get-tuple-element.16), channel_id=1, source_target_pairs={{0,12},{4,24},{8,28},{12,0},{16,20},{20,16},{24,4},{28,8},{1,13},{... | collective-permute-start | bytes 245768 | tf_op jit(solution)/shard_map/ppermute | solution.py:183
  8.5 11.0 %collective-permute-start.3 = (bf16[32,1280]{1,0:T(8,128)(2,1)S(1)}, bf16[32,1280]{1,0:T(8,128)(2,1)S(1)}, u32[]{:S(2)}, u32[]{:S(2)}) collective-permute-start(bf16[32,1280]{1,0:T(8,128)(2,1)S(1)} %get-tuple-element.17), channel_id=1, source_target_pairs={{0,28},{4,12},{8,20},{12,4},{16,24},{20,8},{24,16},{28,0},{1,29},{... | collective-permute-start | bytes 245768 | tf_op jit(solution)/shard_map/ppermute | solution.py:183
  10.7 12.6 %copy-start.1 = (f32[1,1024]{1,0:T(1,128)S(1)}, f32[1,1024]{1,0:T(1,128)}, u32[]{:S(2)}) copy-start(f32[1,1024]{1,0:T(1,128)} %precision_ref.1) | copy-start | bytes 12292
  10.7 12.6 %copy-start = (f32[1,1024]{1,0:T(1,128)S(1)}, f32[1,1024]{1,0:T(1,128)}, u32[]{:S(2)}) copy-start(f32[1,1024]{1,0:T(1,128)} %departure_ref.1) | copy-start | bytes 12292
  10.7 9.0 %collective-permute-start.4 = (bf16[32,1280]{1,0:T(8,128)(2,1)S(1)}, bf16[32,1280]{1,0:T(8,128)(2,1)S(1)}, u32[]{:S(2)}, u32[]{:S(2)}) collective-permute-start(bf16[32,1280]{1,0:T(8,128)(2,1)S(1)} %get-tuple-element.18), channel_id=1, source_target_pairs={{0,16},{4,8},{8,4},{12,24},{16,0},{20,28},{24,12},{28,20},{1,17},{... | collective-permute-start | bytes 245768 | tf_op jit(solution)/shard_map/ppermute | solution.py:183
  12.1 7.6 %collective-permute-start.5 = (bf16[32,1280]{1,0:T(8,128)(2,1)S(1)}, bf16[32,1280]{1,0:T(8,128)(2,1)S(1)}, u32[]{:S(2)}, u32[]{:S(2)}) collective-permute-start(bf16[32,1280]{1,0:T(8,128)(2,1)S(1)} %get-tuple-element.19), channel_id=1, source_target_pairs={{0,4},{4,0},{8,12},{12,8},{16,28},{20,24},{24,20},{28,16},{1,5},{5... | collective-permute-start | bytes 245768 | tf_op jit(solution)/shard_map/ppermute | solution.py:183
  18.8 4.4 %collective-permute-start.6 = (bf16[32,1280]{1,0:T(8,128)(2,1)S(1)}, bf16[32,1280]{1,0:T(8,128)(2,1)S(1)}, u32[]{:S(2)}, u32[]{:S(2)}) collective-permute-start(bf16[32,1280]{1,0:T(8,128)(2,1)S(1)} %get-tuple-element.20), channel_id=1, source_target_pairs={{0,8},{4,20},{8,0},{12,16},{16,12},{20,4},{24,28},{28,24},{1,9},{5... | collective-permute-start | bytes 245768 | tf_op jit(solution)/shard_map/ppermute | solution.py:183

commit v6 on v5

--- a/solution.py
+++ b/solution.py
@@ -83,9 +83,10 @@
         patch = jnp.where(block == k + 1, partner_of(partners, me_ref[0]), patch)
     target = (row % own) * patches + patch
     pick = jnp.where(column == target, F32(1), F32(0)).astype(BF16)
-    for source, place, copy in ((mapped_vmem, unknowns, mapped_copy), (prior_vmem, 0, prior_copy)):
+    mapped_copy.wait()
+    prior_copy.wait()
+    for source, place in ((mapped_vmem, unknowns), (prior_vmem, 0)):
         width = source.shape[2]
-        copy.wait()
         moved = mm(pick, source[...].reshape(size, width)).astype(BF16)
         for s, out_ref in enumerate(out_refs):
             out_ref[:, place : place + width] = moved[s * own : (s + 1) * own]

time: 37.3 us -> 37.1 us (level)
  no operation moved by 1% of the time
where the time goes in v6:
time: 37.1 us; the launch traced here: 36.9 us
  starting transfers between devices  12.5 us (34%)
  blocking collectives  10.5 us (28%)
  waiting for transfers between devices  8.43 us (23%)
  Pallas kernels  4.1 us (11%)
  local copies, waits for them, and re-layouts  0.74 us (2%)
  between operations  0.69 us (2%)
    ppermute x7, starting transfers between devices, local_pairs(): arrived.append(lax.ppermute(blocks[k], 'mem', list(enumerate(partners))))  12.5 us
    all_to_all x1, blocking collectives, local_pairs(): lax.all_to_all(result, 'mem', split_axis=0, concat_axis=0, tiled=True)  10.5 us
    ppermute x7, waiting for transfers between devices, local_pairs(): arrived.append(lax.ppermute(blocks[k], 'mem', list(enumerate(partners))))  8.43 us
    pallas_call x1, Pallas kernels, analyse(): pl.pallas_call(functools.partial(analysis_kernel, unknowns), out_shape=ja...  2.67 us
    pallas_call x1, Pallas kernels, local_pairs(): pl.pallas_call(pack_kernel, out_shape=[jax.ShapeDtypeStruct((own, width),...  1.42 us
  transfers between devices with their start and end apart: 7, of which 3 were waited for; matrix products, arithmetic and copies ran while one was open for 0% of the time, Pallas kernels for 0%

profile of v6, /device:TPU:0, one launch (start us, length us, event | category | flops | bytes accessed | tf_op | source)
XLA Modules:
  0.0 36.9 jit_solution(18341514137520712064)
XLA Ops:
  0.0 1.4 %shard_map.55 = (bf16[32,1280]{1,0:T(8,128)(2,1)S(1)}, bf16[32,1280]{1,0:T(8,128)(2,1)S(1)}, bf16[32,1280]{1,0:T(8,128)(2,1)S(1)}, bf16[32,1280]{1,0:T(8,128)(2,...) custom-call(s32[1]{0:T(128)} %bitcast.me_ref, ...), custom_call_target="tpu_custom_call" | custom-call | tf_op jit(solution)/shard_map/pallas_call | solution.py:166
  1.4 5.1 %collective-permute-start = (bf16[32,1280]{1,0:T(8,128)(2,1)S(1)}, bf16[32,1280]{1,0:T(8,128)(2,1)S(1)}, u32[]{:S(2)}, u32[]{:S(2)}) collective-permute-start(bf16[32,1280]{1,0:T(8,128)(2,1)S(1)} %get-tuple-element.14), channel_id=1, source_target_pairs={{0,24},{4,28},{8,16},{12,20},{16,8},{20,12},{24,0},{28,4},{1,25},{... | collective-permute-start | bytes 245768 | tf_op jit(solution)/shard_map/ppermute | solution.py:184
  6.6 0.4 collective-permute-start.1
  6.9 1.3 %collective-permute-start.2 = (bf16[32,1280]{1,0:T(8,128)(2,1)S(1)}, bf16[32,1280]{1,0:T(8,128)(2,1)S(1)}, u32[]{:S(2)}, u32[]{:S(2)}) collective-permute-start(bf16[32,1280]{1,0:T(8,128)(2,1)S(1)} %get-tuple-element.16), channel_id=1, source_target_pairs={{0,12},{4,24},{8,28},{12,0},{16,20},{20,16},{24,4},{28,8},{1,13},{... | collective-permute-start | bytes 245768 | tf_op jit(solution)/shard_map/ppermute | solution.py:184
  8.3 2.2 %collective-permute-start.3 = (bf16[32,1280]{1,0:T(8,128)(2,1)S(1)}, bf16[32,1280]{1,0:T(8,128)(2,1)S(1)}, u32[]{:S(2)}, u32[]{:S(2)}) collective-permute-start(bf16[32,1280]{1,0:T(8,128)(2,1)S(1)} %get-tuple-element.17), channel_id=1, source_target_pairs={{0,28},{4,12},{8,20},{12,4},{16,24},{20,8},{24,16},{28,0},{1,29},{... | collective-permute-start | bytes 245768 | tf_op jit(solution)/shard_map/ppermute | solution.py:184
  10.5 0.0 copy-start.1
  10.5 0.0 copy-start
  10.5 1.4 %collective-permute-start.4 = (bf16[32,1280]{1,0:T(8,128)(2,1)S(1)}, bf16[32,1280]{1,0:T(8,128)(2,1)S(1)}, u32[]{:S(2)}, u32[]{:S(2)}) collective-permute-start(bf16[32,1280]{1,0:T(8,128)(2,1)S(1)} %get-tuple-element.18), channel_id=1, source_target_pairs={{0,16},{4,8},{8,4},{12,24},{16,0},{20,28},{24,12},{28,20},{1,17},{... | collective-permute-start | bytes 245768 | tf_op jit(solution)/shard_map/ppermute | solution.py:184
  11.9 0.0 collective-permute-done.refs_1_
  11.9 2.0 %collective-permute-start.5 = (bf16[32,1280]{1,0:T(8,128)(2,1)S(1)}, bf16[32,1280]{1,0:T(8,128)(2,1)S(1)}, u32[]{:S(2)}, u32[]{:S(2)}) collective-permute-start(bf16[32,1280]{1,0:T(8,128)(2,1)S(1)} %get-tuple-element.19), channel_id=1, source_target_pairs={{0,4},{4,0},{8,12},{12,8},{16,28},{20,24},{24,20},{28,16},{1,5},{5... | collective-permute-start | bytes 245768 | tf_op jit(solution)/shard_map/ppermute | solution.py:184
  13.9 4.7 %collective-permute-done.1.refs_2_ = bf16[32,1280]{1,0:T(8,128)(2,1)S(1)} collective-permute-done((bf16[32,1280]{1,0:T(8,128)(2,1)S(1)}, bf16[32,1280]{1,0:T(8,128)(2,1)S(1)}, u32[]{:S(2)}, u32[]{:S(2)}) %collective-permute-start.1) | collective-permute-done | bytes 81952 | tf_op jit(solution)/shard_map/ppermute | solution.py:184
  18.6 0.0 collective-permute-start.6
  19.2 0.0 collective-permute-done.2.refs_3_
  19.2 0.0 collective-permute-done.3.refs_4_
  19.3 0.2 collective-permute-done.4.refs_5_
  19.5 0.0 collective-permute-done.5.refs_6_
  19.5 3.5 %collective-permute-done.6.refs_7_ = bf16[32,1280]{1,0:T(8,128)(2,1)S(1)} collective-permute-done((bf16[32,1280]{1,0:T(8,128)(2,1)S(1)}, bf16[32,1280]{1,0:T(8,128)(2,1)S(1)}, u32[]{:S(2)}, u32[]{:S(2)}) %collective-permute-start.6) | collective-permute-done | bytes 81952 | tf_op jit(solution)/shard_map/ppermute | solution.py:184
  23.0 0.0 copy-done.1
  23.0 0.0 copy-done
  23.0 2.7 %shard_map.56 = bf16[8,32,256]{2,1,0:T(8,128)(2,1)S(1)} custom-call(s32[1]{0:T(128)} %bitcast.me_ref, s32[1]{0:T(128)S(6)} %copy.7.lines_ref, f32[1,1024]{1,0:T(1,128)S(1)} %copy-done, f32[1,1024]{1,0:T(1,128)S(1)} %copy-done.1, bf16[32,1280]{1,0:T(8,128)(2,1)S(1)} %get-tuple-element.13.refs_0_, bf16[32,1280]{1,0:T(8,128)(2,1)S(1)} %collective-permute-done.refs_1_, ...), custom_call_target="tpu_custom_call" | custom-call | tf_op jit(solution)/shard_map/pallas_call | solution.py:153
  25.7 10.5 %all_to_all.5 = bf16[8,32,256]{2,1,0:T(8,128)(2,1)S(1)} all-to-all(bf16[8,32,256]{2,1,0:T(8,128)(2,1)S(1)} %shard_map.56), channel_id=1, replica_groups=mesh['mem'=8,'grp'=4] {'mem'}, dimensions={0} | all-to-all | bytes 262144 | tf_op jit(solution)/shard_map/all_to_all | solution.py:186
  36.2 0.7 %copy.6 = bf16[32,8,256]{2,1,0:T(8,128)(2,1)} copy(bf16[32,8,256]{2,0,1:T(8,128)(2,1)S(1)} %bitcast.2) | data formatting | bytes 262144 | tf_op jit(solution)/shard_map/transpose | solution.py:187
Async XLA Ops:
  1.4 10.5 %collective-permute-start = (bf16[32,1280]{1,0:T(8,128)(2,1)S(1)}, bf16[32,1280]{1,0:T(8,128)(2,1)S(1)}, u32[]{:S(2)}, u32[]{:S(2)}) collective-permute-start(bf16[32,1280]{1,0:T(8,128)(2,1)S(1)} %get-tuple-element.14), channel_id=1, source_target_pairs={{0,24},{4,28},{8,16},{12,20},{16,8},{20,12},{24,0},{28,4},{1,25},{... | collective-permute-start | bytes 245768 | tf_op jit(solution)/shard_map/ppermute | solution.py:184
  6.6 12.0 %collective-permute-start.1 = (bf16[32,1280]{1,0:T(8,128)(2,1)S(1)}, bf16[32,1280]{1,0:T(8,128)(2,1)S(1)}, u32[]{:S(2)}, u32[]{:S(2)}) collective-permute-start(bf16[32,1280]{1,0:T(8,128)(2,1)S(1)} %get-tuple-element.15), channel_id=1, source_target_pairs={{0,20},{4,16},{8,24},{12,28},{16,4},{20,0},{24,8},{28,12},{1,21},{... | collective-permute-start | bytes 245768 | tf_op jit(solution)/shard_map/ppermute | solution.py:184
  6.9 12.3 %collective-permute-start.2 = (bf16[32,1280]{1,0:T(8,128)(2,1)S(1)}, bf16[32,1280]{1,0:T(8,128)(2,1)S(1)}, u32[]{:S(2)}, u32[]{:S(2)}) collective-permute-start(bf16[32,1280]{1,0:T(8,128)(2,1)S(1)} %get-tuple-element.16), channel_id=1, source_target_pairs={{0,12},{4,24},{8,28},{12,0},{16,20},{20,16},{24,4},{28,8},{1,13},{... | collective-permute-start | bytes 245768 | tf_op jit(solution)/shard_map/ppermute | solution.py:184
  8.3 11.0 %collective-permute-start.3 = (bf16[32,1280]{1,0:T(8,128)(2,1)S(1)}, bf16[32,1280]{1,0:T(8,128)(2,1)S(1)}, u32[]{:S(2)}, u32[]{:S(2)}) collective-permute-start(bf16[32,1280]{1,0:T(8,128)(2,1)S(1)} %get-tuple-element.17), channel_id=1, source_target_pairs={{0,28},{4,12},{8,20},{12,4},{16,24},{20,8},{24,16},{28,0},{1,29},{... | collective-permute-start | bytes 245768 | tf_op jit(solution)/shard_map/ppermute | solution.py:184
  10.5 12.5 %copy-start.1 = (f32[1,1024]{1,0:T(1,128)S(1)}, f32[1,1024]{1,0:T(1,128)}, u32[]{:S(2)}) copy-start(f32[1,1024]{1,0:T(1,128)} %precision_ref.1) | copy-start | bytes 12292
  10.5 12.5 %copy-start = (f32[1,1024]{1,0:T(1,128)S(1)}, f32[1,1024]{1,0:T(1,128)}, u32[]{:S(2)}) copy-start(f32[1,1024]{1,0:T(1,128)} %departure_ref.1) | copy-start | bytes 12292
  10.5 9.0 %collective-permute-start.4 = (bf16[32,1280]{1,0:T(8,128)(2,1)S(1)}, bf16[32,1280]{1,0:T(8,128)(2,1)S(1)}, u32[]{:S(2)}, u32[]{:S(2)}) collective-permute-start(bf16[32,1280]{1,0:T(8,128)(2,1)S(1)} %get-tuple-element.18), channel_id=1, source_target_pairs={{0,16},{4,8},{8,4},{12,24},{16,0},{20,28},{24,12},{28,20},{1,17},{... | collective-permute-start | bytes 245768 | tf_op jit(solution)/shard_map/ppermute | solution.py:184
  11.9 7.6 %collective-permute-start.5 = (bf16[32,1280]{1,0:T(8,128)(2,1)S(1)}, bf16[32,1280]{1,0:T(8,128)(2,1)S(1)}, u32[]{:S(2)}, u32[]{:S(2)}) collective-permute-start(bf16[32,1280]{1,0:T(8,128)(2,1)S(1)} %get-tuple-element.19), channel_id=1, source_target_pairs={{0,4},{4,0},{8,12},{12,8},{16,28},{20,24},{24,20},{28,16},{1,5},{5... | collective-permute-start | bytes 245768 | tf_op jit(solution)/shard_map/ppermute | solution.py:184
  18.6 4.4 %collective-permute-start.6 = (bf16[32,1280]{1,0:T(8,128)(2,1)S(1)}, bf16[32,1280]{1,0:T(8,128)(2,1)S(1)}, u32[]{:S(2)}, u32[]{:S(2)}) collective-permute-start(bf16[32,1280]{1,0:T(8,128)(2,1)S(1)} %get-tuple-element.20), channel_id=1, source_target_pairs={{0,8},{4,20},{8,0},{12,16},{16,12},{20,4},{24,28},{28,24},{1,9},{5... | collective-permute-start | bytes 245768 | tf_op jit(solution)/shard_map/ppermute | solution.py:184

commit v7 on v6

--- a/solution.py
+++ b/solution.py
@@ -106,7 +106,7 @@
     root_weights = jnp.sqrt(weights)
     scaled = deviat * root_weights
     scaled = scaled.astype(BF16)
-    gram = mm(scaled, scaled, (1, 1))
+    gram = mm(scaled, scaled.T)
     pull = scaled.astype(F32) * (root_weights * departure_ref[...])
     pull = jnp.sum(pull, axis=1, keepdims=True)
 
@@ -121,7 +121,7 @@
     norm2 = jnp.sum(jnp.sum(system * system, axis=0, keepdims=True), axis=1, keepdims=True)
     inv_scale = lax.rsqrt(norm2)
     product = system.astype(BF16)
-    square = right(system, product)
+    square = mm(product, product)
     root = jnp.where(rows == columns, F32(1.5), 0.0) - 0.5 * inv_scale * product.astype(F32)
     iterate = inv_scale * (1.5 * system - 0.5 * inv_scale * square)
     for _ in range(1, ITERS - 1):
@@ -129,7 +129,7 @@
         iterate = 1.5 * iterate - 0.5 * right(iterate, product)
         root = 1.5 * root - 0.5 * left(product, root)
     product = mm3(root, iterate)
-    moved = right(root, spread.astype(BF16))
+    moved = mm3(root, spread)
     moved = 1.5 * moved - 0.5 * mm3(product, moved)
     pull = times(root, pull)
     pull = 1.5 * pull - 0.5 * times(product, pull)

time: 37.1 us -> 37.1 us (level)
  no operation moved by 1% of the time
where the time goes in v7:
time: 37.1 us; the launch traced here: 36.9 us
  starting transfers between devices  12.5 us (34%)
  blocking collectives  10.5 us (28%)
  waiting for transfers between devices  8.43 us (23%)
  Pallas kernels  4.08 us (11%)
  local copies, waits for them, and re-layouts  0.74 us (2%)
  between operations  0.69 us (2%)
    ppermute x7, starting transfers between devices, local_pairs(): arrived.append(lax.ppermute(blocks[k], 'mem', list(enumerate(partners))))  12.5 us
    all_to_all x1, blocking collectives, local_pairs(): lax.all_to_all(result, 'mem', split_axis=0, concat_axis=0, tiled=True)  10.5 us
    ppermute x7, waiting for transfers between devices, local_pairs(): arrived.append(lax.ppermute(blocks[k], 'mem', list(enumerate(partners))))  8.43 us
    pallas_call x1, Pallas kernels, analyse(): pl.pallas_call(functools.partial(analysis_kernel, unknowns), out_shape=ja...  2.65 us
    pallas_call x1, Pallas kernels, local_pairs(): pl.pallas_call(pack_kernel, out_shape=[jax.ShapeDtypeStruct((own, width),...  1.42 us
  transfers between devices with their start and end apart: 7, of which 3 were waited for; matrix products, arithmetic and copies ran while one was open for 0% of the time, Pallas kernels for 0%

profile of v7, /device:TPU:0, one launch (start us, length us, event | category | flops | bytes accessed | tf_op | source)
XLA Modules:
  0.0 36.9 jit_solution(283045526196093224)
XLA Ops:
  0.0 1.4 %shard_map.55 = (bf16[32,1280]{1,0:T(8,128)(2,1)S(1)}, bf16[32,1280]{1,0:T(8,128)(2,1)S(1)}, bf16[32,1280]{1,0:T(8,128)(2,1)S(1)}, bf16[32,1280]{1,0:T(8,128)(2,...) custom-call(s32[1]{0:T(128)} %bitcast.me_ref, ...), custom_call_target="tpu_custom_call" | custom-call | tf_op jit(solution)/shard_map/pallas_call | solution.py:166
  1.4 5.1 %collective-permute-start = (bf16[32,1280]{1,0:T(8,128)(2,1)S(1)}, bf16[32,1280]{1,0:T(8,128)(2,1)S(1)}, u32[]{:S(2)}, u32[]{:S(2)}) collective-permute-start(bf16[32,1280]{1,0:T(8,128)(2,1)S(1)} %get-tuple-element.14), channel_id=1, source_target_pairs={{0,24},{4,28},{8,16},{12,20},{16,8},{20,12},{24,0},{28,4},{1,25},{... | collective-permute-start | bytes 245768 | tf_op jit(solution)/shard_map/ppermute | solution.py:184
  6.6 0.4 collective-permute-start.1
  6.9 1.3 %collective-permute-start.2 = (bf16[32,1280]{1,0:T(8,128)(2,1)S(1)}, bf16[32,1280]{1,0:T(8,128)(2,1)S(1)}, u32[]{:S(2)}, u32[]{:S(2)}) collective-permute-start(bf16[32,1280]{1,0:T(8,128)(2,1)S(1)} %get-tuple-element.16), channel_id=1, source_target_pairs={{0,12},{4,24},{8,28},{12,0},{16,20},{20,16},{24,4},{28,8},{1,13},{... | collective-permute-start | bytes 245768 | tf_op jit(solution)/shard_map/ppermute | solution.py:184
  8.3 2.2 %collective-permute-start.3 = (bf16[32,1280]{1,0:T(8,128)(2,1)S(1)}, bf16[32,1280]{1,0:T(8,128)(2,1)S(1)}, u32[]{:S(2)}, u32[]{:S(2)}) collective-permute-start(bf16[32,1280]{1,0:T(8,128)(2,1)S(1)} %get-tuple-element.17), channel_id=1, source_target_pairs={{0,28},{4,12},{8,20},{12,4},{16,24},{20,8},{24,16},{28,0},{1,29},{... | collective-permute-start | bytes 245768 | tf_op jit(solution)/shard_map/ppermute | solution.py:184
  10.5 0.0 copy-start.1
  10.5 0.0 copy-start
  10.5 1.4 %collective-permute-start.4 = (bf16[32,1280]{1,0:T(8,128)(2,1)S(1)}, bf16[32,1280]{1,0:T(8,128)(2,1)S(1)}, u32[]{:S(2)}, u32[]{:S(2)}) collective-permute-start(bf16[32,1280]{1,0:T(8,128)(2,1)S(1)} %get-tuple-element.18), channel_id=1, source_target_pairs={{0,16},{4,8},{8,4},{12,24},{16,0},{20,28},{24,12},{28,20},{1,17},{... | collective-permute-start | bytes 245768 | tf_op jit(solution)/shard_map/ppermute | solution.py:184
  11.9 0.0 collective-permute-done.refs_1_
  11.9 2.0 %collective-permute-start.5 = (bf16[32,1280]{1,0:T(8,128)(2,1)S(1)}, bf16[32,1280]{1,0:T(8,128)(2,1)S(1)}, u32[]{:S(2)}, u32[]{:S(2)}) collective-permute-start(bf16[32,1280]{1,0:T(8,128)(2,1)S(1)} %get-tuple-element.19), channel_id=1, source_target_pairs={{0,4},{4,0},{8,12},{12,8},{16,28},{20,24},{24,20},{28,16},{1,5},{5... | collective-permute-start | bytes 245768 | tf_op jit(solution)/shard_map/ppermute | solution.py:184
  13.9 4.7 %collective-permute-done.1.refs_2_ = bf16[32,1280]{1,0:T(8,128)(2,1)S(1)} collective-permute-done((bf16[32,1280]{1,0:T(8,128)(2,1)S(1)}, bf16[32,1280]{1,0:T(8,128)(2,1)S(1)}, u32[]{:S(2)}, u32[]{:S(2)}) %collective-permute-start.1) | collective-permute-done | bytes 81952 | tf_op jit(solution)/shard_map/ppermute | solution.py:184
  18.6 0.0 collective-permute-start.6
  19.2 0.0 collective-permute-done.2.refs_3_
  19.2 0.0 collective-permute-done.3.refs_4_
  19.3 0.2 collective-permute-done.4.refs_5_
  19.5 0.0 collective-permute-done.5.refs_6_
  19.5 3.5 %collective-permute-done.6.refs_7_ = bf16[32,1280]{1,0:T(8,128)(2,1)S(1)} collective-permute-done((bf16[32,1280]{1,0:T(8,128)(2,1)S(1)}, bf16[32,1280]{1,0:T(8,128)(2,1)S(1)}, u32[]{:S(2)}, u32[]{:S(2)}) %collective-permute-start.6) | collective-permute-done | bytes 81952 | tf_op jit(solution)/shard_map/ppermute | solution.py:184
  23.0 0.0 copy-done.1
  23.0 0.0 copy-done
  23.0 2.7 %shard_map.56 = bf16[8,32,256]{2,1,0:T(8,128)(2,1)S(1)} custom-call(s32[1]{0:T(128)} %bitcast.me_ref, s32[1]{0:T(128)S(6)} %copy.7.lines_ref, f32[1,1024]{1,0:T(1,128)S(1)} %copy-done, f32[1,1024]{1,0:T(1,128)S(1)} %copy-done.1, bf16[32,1280]{1,0:T(8,128)(2,1)S(1)} %get-tuple-element.13.refs_0_, bf16[32,1280]{1,0:T(8,128)(2,1)S(1)} %collective-permute-done.refs_1_, ...), custom_call_target="tpu_custom_call" | custom-call | tf_op jit(solution)/shard_map/pallas_call | solution.py:153
  25.7 10.5 %all_to_all.5 = bf16[8,32,256]{2,1,0:T(8,128)(2,1)S(1)} all-to-all(bf16[8,32,256]{2,1,0:T(8,128)(2,1)S(1)} %shard_map.56), channel_id=1, replica_groups=mesh['mem'=8,'grp'=4] {'mem'}, dimensions={0} | all-to-all | bytes 262144 | tf_op jit(solution)/shard_map/all_to_all | solution.py:186
  36.1 0.7 %copy.6 = bf16[32,8,256]{2,1,0:T(8,128)(2,1)} copy(bf16[32,8,256]{2,0,1:T(8,128)(2,1)S(1)} %bitcast.2) | data formatting | bytes 262144 | tf_op jit(solution)/shard_map/transpose | solution.py:187
Async XLA Ops:
  1.4 10.5 %collective-permute-start = (bf16[32,1280]{1,0:T(8,128)(2,1)S(1)}, bf16[32,1280]{1,0:T(8,128)(2,1)S(1)}, u32[]{:S(2)}, u32[]{:S(2)}) collective-permute-start(bf16[32,1280]{1,0:T(8,128)(2,1)S(1)} %get-tuple-element.14), channel_id=1, source_target_pairs={{0,24},{4,28},{8,16},{12,20},{16,8},{20,12},{24,0},{28,4},{1,25},{... | collective-permute-start | bytes 245768 | tf_op jit(solution)/shard_map/ppermute | solution.py:184
  6.6 12.0 %collective-permute-start.1 = (bf16[32,1280]{1,0:T(8,128)(2,1)S(1)}, bf16[32,1280]{1,0:T(8,128)(2,1)S(1)}, u32[]{:S(2)}, u32[]{:S(2)}) collective-permute-start(bf16[32,1280]{1,0:T(8,128)(2,1)S(1)} %get-tuple-element.15), channel_id=1, source_target_pairs={{0,20},{4,16},{8,24},{12,28},{16,4},{20,0},{24,8},{28,12},{1,21},{... | collective-permute-start | bytes 245768 | tf_op jit(solution)/shard_map/ppermute | solution.py:184
  6.9 12.3 %collective-permute-start.2 = (bf16[32,1280]{1,0:T(8,128)(2,1)S(1)}, bf16[32,1280]{1,0:T(8,128)(2,1)S(1)}, u32[]{:S(2)}, u32[]{:S(2)}) collective-permute-start(bf16[32,1280]{1,0:T(8,128)(2,1)S(1)} %get-tuple-element.16), channel_id=1, source_target_pairs={{0,12},{4,24},{8,28},{12,0},{16,20},{20,16},{24,4},{28,8},{1,13},{... | collective-permute-start | bytes 245768 | tf_op jit(solution)/shard_map/ppermute | solution.py:184
  8.3 11.0 %collective-permute-start.3 = (bf16[32,1280]{1,0:T(8,128)(2,1)S(1)}, bf16[32,1280]{1,0:T(8,128)(2,1)S(1)}, u32[]{:S(2)}, u32[]{:S(2)}) collective-permute-start(bf16[32,1280]{1,0:T(8,128)(2,1)S(1)} %get-tuple-element.17), channel_id=1, source_target_pairs={{0,28},{4,12},{8,20},{12,4},{16,24},{20,8},{24,16},{28,0},{1,29},{... | collective-permute-start | bytes 245768 | tf_op jit(solution)/shard_map/ppermute | solution.py:184
  10.5 12.5 %copy-start.1 = (f32[1,1024]{1,0:T(1,128)S(1)}, f32[1,1024]{1,0:T(1,128)}, u32[]{:S(2)}) copy-start(f32[1,1024]{1,0:T(1,128)} %precision_ref.1) | copy-start | bytes 12292
  10.5 12.5 %copy-start = (f32[1,1024]{1,0:T(1,128)S(1)}, f32[1,1024]{1,0:T(1,128)}, u32[]{:S(2)}) copy-start(f32[1,1024]{1,0:T(1,128)} %departure_ref.1) | copy-start | bytes 12292
  10.5 9.0 %collective-permute-start.4 = (bf16[32,1280]{1,0:T(8,128)(2,1)S(1)}, bf16[32,1280]{1,0:T(8,128)(2,1)S(1)}, u32[]{:S(2)}, u32[]{:S(2)}) collective-permute-start(bf16[32,1280]{1,0:T(8,128)(2,1)S(1)} %get-tuple-element.18), channel_id=1, source_target_pairs={{0,16},{4,8},{8,4},{12,24},{16,0},{20,28},{24,12},{28,20},{1,17},{... | collective-permute-start | bytes 245768 | tf_op jit(solution)/shard_map/ppermute | solution.py:184
  11.9 7.6 %collective-permute-start.5 = (bf16[32,1280]{1,0:T(8,128)(2,1)S(1)}, bf16[32,1280]{1,0:T(8,128)(2,1)S(1)}, u32[]{:S(2)}, u32[]{:S(2)}) collective-permute-start(bf16[32,1280]{1,0:T(8,128)(2,1)S(1)} %get-tuple-element.19), channel_id=1, source_target_pairs={{0,4},{4,0},{8,12},{12,8},{16,28},{20,24},{24,20},{28,16},{1,5},{5... | collective-permute-start | bytes 245768 | tf_op jit(solution)/shard_map/ppermute | solution.py:184
  18.6 4.4 %collective-permute-start.6 = (bf16[32,1280]{1,0:T(8,128)(2,1)S(1)}, bf16[32,1280]{1,0:T(8,128)(2,1)S(1)}, u32[]{:S(2)}, u32[]{:S(2)}) collective-permute-start(bf16[32,1280]{1,0:T(8,128)(2,1)S(1)} %get-tuple-element.20), channel_id=1, source_target_pairs={{0,8},{4,20},{8,0},{12,16},{16,12},{20,4},{24,28},{28,24},{1,9},{5... | collective-permute-start | bytes 245768 | tf_op jit(solution)/shard_map/ppermute | solution.py:184
